TPU v7x, 128 devices: a whole 4x4x4 slice. The times are simulated.
128 devices in a mesh: req: 32 (over y, z, core), tensor: 4 (over x).
Axes of the slice: x: 4, y: 4, z: 4, core: 2. Of those that a mesh axis runs over, the one named last changes fastest.
Arguments:
- hidden: bfloat16 [32768, 1024], P('req', 'tensor')
- gain: bfloat16 [1024], P('tensor'), may hold values from 0.5 to 1.5
- head: bfloat16 [1024, 32128], P(None, ('req', 'tensor'))
- token_ids: int32 [32768], P('req'), may hold values from 0 to 32127
- lengths: int32 [32], P('req'), may hold values from 1 to 1024, 12288 in all
- prompt_of: int32 [32], P('req'), may hold values from 0 to 3, as said below
Outputs:
- token_logprob: float32 [32768], P(('req', 'tensor'))
- token_entropy: float32 [32768], P(('req', 'tensor'))
- prompt_stats: float32 [4, 2], replicated
Inputs may be any that keep to these rules, and one draw needn't show every extreme that they name: The lengths sum to 12288 and the longest is exactly 1024. `prompt_of`: a prompt may have no responses.
All inputs are finite; a program needn't handle non-finite values. No bound on the sum of `lengths` on one device may be relied on, other than what follows from the above.
Results may differ from a plain program's by a relative error of at most 0.0019.
Values may be sent and summed in bfloat16 or wider, within the bound.
A program may use at most 128 MiB of HBM per device.

v0:
```python
import jax
import jax.numpy as jnp
from jax import lax
from jax.sharding import PartitionSpec as P
from jax.experimental.layout import Layout, with_layout_constraint

PROMPTS = 4
NEG = -1e30

eps = 1e-06


def chunk_stats(normed, piece, vocab_ids, valid, ids):
    logits = lax.dot_general(normed, piece, (((1,), (1,)), ((), ())), preferred_element_type=jnp.float32)
    logits = jnp.where(valid[None, :], logits, NEG)
    top = jnp.max(logits, axis=1)
    expo = jnp.exp(logits - top[:, None])
    total = jnp.sum(expo, axis=1)
    moment = jnp.sum(expo * logits, axis=1)
    pick = jnp.sum(jnp.where(vocab_ids[None, :] == ids[:, None], logits, 0.0), axis=1)
    return top, total, moment, pick


def merge(stats):
    tops = jnp.stack([s[0] for s in stats])
    top = jnp.max(tops, axis=0)
    factor = jnp.exp(tops - top[None, :])
    total = jnp.sum(factor * jnp.stack([s[1] for s in stats]), axis=0)
    moment = jnp.sum(factor * jnp.stack([s[2] for s in stats]), axis=0)
    pick = jnp.sum(jnp.stack([s[3] for s in stats]), axis=0)
    return top, total, moment, pick


def body(hidden, gain, head, token_ids, lengths, prompt_of):
    rows, part_width = hidden.shape
    splits = lax.axis_size("tensor")
    column_index = lax.axis_index("tensor")
    req_count = lax.axis_size("req")
    shard_cols = head.shape[1]
    width = part_width * splits

    extra = jnp.zeros((8, part_width), hidden.dtype).at[0].set(gain)
    packed = jnp.concatenate([hidden, extra], axis=0)
    stacked = lax.all_gather(packed, "tensor", axis=0, tiled=False)
    gathered = jnp.transpose(stacked, (1, 0, 2)).reshape(rows + 8, width)
    widened = gathered[:rows].astype(jnp.float32)
    gain_full = gathered[rows].astype(jnp.float32)
    scale = lax.rsqrt(jnp.sum(widened * widened, axis=1) / width + eps)
    normed = (widened * scale[:, None] * gain_full[None, :]).astype(jnp.bfloat16)

    chunk = 128
    bounds = [(lo, min(lo + chunk, shard_cols)) for lo in range(0, shard_cols, chunk)]
    stats = []
    for lo, hi in bounds:
        part = head[:, lo:hi].T
        if hi - lo < chunk:
            part = jnp.concatenate([part, jnp.zeros((chunk - (hi - lo), part.shape[1]), part.dtype)], axis=0)
        part = with_layout_constraint(part, Layout(major_to_minor=(0, 1)))
        piece = lax.all_gather(part, "req", axis=0, tiled=False)
        piece = with_layout_constraint(piece, Layout(major_to_minor=(0, 1, 2)))
        piece = piece.reshape(req_count * chunk, piece.shape[2])
        g = jnp.arange(req_count * chunk, dtype=jnp.int32)
        owner = g // chunk
        offset = lo + g % chunk
        valid = offset < hi
        vocab_ids = jnp.where(valid, (owner * splits + column_index) * shard_cols + offset, -1)
        stats.append(chunk_stats(normed, piece, vocab_ids, valid, token_ids))
    mine = merge(stats)

    everyone = lax.all_gather(jnp.stack(mine), "tensor", axis=0, tiled=False)
    top, total, moment, picked = merge([tuple(everyone[k, j] for j in range(4)) for k in range(splits)])

    positions = jnp.arange(rows, dtype=jnp.int32)
    live = positions < lengths[0]
    safe_total = jnp.where(live, total, 1.0)
    log_norm = top + jnp.log(safe_total)
    logprob = jnp.where(live, picked - log_norm, 0.0)
    entropy = jnp.where(live, log_norm - moment / safe_total, 0.0)
    onehot = (jnp.arange(PROMPTS, dtype=jnp.int32) == prompt_of[0]).astype(jnp.float32)
    share = rows // splits
    own_logprob = lax.dynamic_slice_in_dim(logprob, column_index * share, share)
    own_entropy = lax.dynamic_slice_in_dim(entropy, column_index * share, share)
    count = jnp.where(column_index == 0, lengths[0], 0).astype(jnp.float32)
    summary = jnp.stack([jnp.sum(own_entropy), jnp.sum(own_logprob), count])
    summed = lax.psum(onehot[:, None] * summary[None, :], ("req", "tensor"))
    prompt_stats = summed[:, :2] / jnp.maximum(summed[:, 2:3], 1.0)
    return (own_logprob, own_entropy, prompt_stats)


def solution(mesh):
    in_specs = (
        P("req", "tensor"),
        P("tensor"),
        P(None, ("req", "tensor")),
        P("req"),
        P("req"),
        P("req"),
    )
    out_specs = (P(("req", "tensor")), P(("req", "tensor")), P())
    return jax.shard_map(body, mesh=mesh, in_specs=in_specs, out_specs=out_specs, check_vma=False)
```

profile of v0, /device:TPU:0, one launch (start us, length us, event | category | flops | bytes accessed | tf_op | source)
XLA Modules:
  0.0 273.6 jit_solution(5163023839343527258)
XLA Ops:
  7.2 0.0 all-gather.9.cloned.1.call-start
  7.2 0.7 reshape.187
  7.9 1.9 fusion.6
  9.8 0.0 all-gather.9.cloned.1.call-update
  9.8 0.0 all-gather.13.cloned.1.call-start
  9.8 1.0 slice.85
  10.8 0.2 copy.24
  11.0 0.7 concatenate.9
  11.7 0.0 all-gather.13.cloned.1.call-update
  11.8 0.0 all-gather.11.cloned.1.call-start
  11.8 1.0 slice.84
  12.8 0.9 copy.23
  13.7 0.0 all-gather.11.cloned.1.call-update
  15.1 28.3 %all-gather.9.cloned.1.call-done = bf16[4128,256]{1,0:T(8,128)(2,1)} async-done(((bf16[1032,256]{1,0:T(8,128)(2,1)}), bf16[4128,256]{1,0:T(8,128)(2,1)}) %all-gather.9.cloned.1.call-update) | async-done | bytes 2113552 | tf_op jit(solution)/shard_map/all_gather | solution.py:44
  43.3 0.7 slice_convert_fusion
  44.0 2.1 fusion.2
  46.1 2.1 fusion.4
  48.3 2.5 copy.19
  50.8 47.7 %all-gather.13.cloned.1.call-done = bf16[4096,1024]{1,0:T(8,128)(2,1)} async-done(((bf16[128,1024]{1,0:T(8,128)(2,1)}), bf16[4096,1024]{1,0:T(8,128)(2,1)}) %all-gather.13.cloned.1.call-update) | async-done | bytes 8388624 | tf_op jit(solution)/shard_map/all_gather | solution.py:59
  98.5 0.0 copy-start
  98.5 16.3 %select_reduce_fusion.2 = (f32[1024]{0:T(1024)S(1)}, f32[1024,4096]{1,0:T(8,128)}) fusion(pred[4096]{0:T(1024)(128)(4,1)S(1)} %fusion.22, bf16[1024,1024]{0,1:T(8,128)(2,1)} %bitcast.69, bf16[4096,1024]{1,0:T(8,128)(2,1)} %all-gather.13.cloned.1.call-done), kind=kOutput, calls=%fused_computation.8 | convolution fusion | flops 8598322176 | bytes 27271168 | tf_op jit(solution)/shard_map/dot_general | solution.py:14
  114.9 0.0 copy-start.1
  114.9 38.3 %all-gather.11.cloned.1.call-done = bf16[4096,1024]{1,0:T(8,128)(2,1)} async-done(((bf16[128,1024]{1,0:T(8,128)(2,1)}), bf16[4096,1024]{1,0:T(8,128)(2,1)}) %all-gather.11.cloned.1.call-update) | async-done | bytes 8388624 | tf_op jit(solution)/shard_map/all_gather | solution.py:59
  153.2 0.0 copy-done
  153.2 14.6 %select_reduce_fusion.3 = (f32[1024]{0:T(1024)S(1)}, f32[1024,4096]{1,0:T(8,128)}) fusion(pred[4096]{0:T(1024)(128)(4,1)S(1)} %fusion.21, bf16[1024,1024]{0,1:T(8,128)(2,1)S(1)} %bitcast.70, bf16[4096,1024]{1,0:T(8,128)(2,1)} %all-gather.11.cloned.1.call-done), kind=kOutput, calls=%fused_computation.9 | convolution fusion | flops 8598322176 | bytes 27271168 | tf_op jit(solution)/shard_map/dot_general | solution.py:14
  167.8 0.0 copy-done.1
  167.8 18.8 %fusion = (f32[1024]{0:T(1024)S(1)}, f32[1024]{0:T(1024)S(1)}, f32[1024]{0:T(1024)S(1)}, f32[1024]{0:T(1024)S(1)}, f32[1024]{0:T(1024)S(1)}, /*index=5*/f32[1024]{0:T(1024)S(1)}) fusion(f32[1024,4096]{1,0:T(8,128)} %get-tuple-element.48, f32[1024]{0:T(1024)S(1)} %get-tuple-element.47, pred[4096]{0:T(1024)(128)(4,1)S(1)} %fusion.22, s32[1024]{0:T(1024)S(1)} %copy-done.1, ...), kind=kLoop, calls=%fused_computation.5 | loop fusion | flops 67102720 | bytes 33632256 | tf_op jit(solution)/shard_map/reduce_sum | solution.py:18
  186.8 12.2 %all-gather.4 = f32[4,4,1024]{2,1,0:T(4,128)S(1)} all-gather(f32[1,4,1024]{2,1,0:T(4,128)S(1)} %maximum_bitcast_fusion), channel_id=5, replica_groups=mesh['req'=32,'tensor'=4] {'tensor'}, dimensions={0}, use_global_device_ids=true | all-gather | bytes 81920 | tf_op jit(solution)/shard_map/all_gather | solution.py:70
  199.0 0.1 fusion.17
  199.1 1.3 fusion.29
  200.4 1.4 pad_maximum_fusion
  201.8 0.1 broadcast_multiply_fusion
  201.9 64.6 %psum.7 = f32[4,3]{0,1:T(4,128)S(1)} all-reduce(f32[4,3]{0,1:T(4,128)S(1)} %broadcast_multiply_fusion), channel_id=1, replica_groups=mesh['req'=32,'tensor'=4] {'req','tensor'}, use_global_device_ids=true, to_apply=%region_15.16 | all-reduce | flops 12 | bytes 96 | tf_op jit(solution)/shard_map/psum | solution.py:85
  266.5 0.6 slice_divide_fusion
  (16 shorter events, 0.2 us)
Async XLA Ops:
  7.2 36.2 %all-gather.9.cloned.1.call-start = ((), (), s32[]{:S(2)}) async-start(), calls=%async_computation | async-start | bytes 2641920 | tf_op jit(solution)/shard_map/all_gather | solution.py:44
  9.8 88.7 %all-gather.13.cloned.1.call-start = ((), (), s32[]{:S(2)}) async-start(), calls=%async_computation.2 | async-start | bytes 8650752 | tf_op jit(solution)/shard_map/all_gather | solution.py:59
  11.8 141.4 %all-gather.11.cloned.1.call-start = ((), (), s32[]{:S(2)}) async-start(), calls=%async_computation.1 | async-start | bytes 8650752 | tf_op jit(solution)/shard_map/all_gather | solution.py:59
  98.5 54.7 %copy-start = (bf16[1024,4,256]{0,2,1:T(8,128)(2,1)S(1)}, bf16[1024,4,256]{0,2,1:T(8,128)(2,1)}, u32[]{:S(2)}) copy-start(bf16[1024,4,256]{0,2,1:T(8,128)(2,1)} %copy.19) | copy-start | bytes 6291460
  114.9 53.0 %copy-start.1 = (s32[1024]{0:T(1024)S(1)}, s32[1024]{0:T(1024)}, u32[]{:S(2)}) copy-start(s32[1024]{0:T(1024)} %param.11) | copy-start | bytes 12292
Sparse Core Ops, SparseCore 0:
  9.9 33.3 all-gather.8
  45.6 52.9 all-gather.12
  100.8 52.3 all-gather.10
where the time goes:
time: 274 us
  waiting for transfers between devices  114 us (42%)
  blocking collectives  76.8 us (28%)
  matrix products  30.9 us (11%)
  other arithmetic  29.3 us (11%)
  between operations  15.2 us (6%)
  local copies, waits for them, and re-layouts  6.94 us (3%)
    all_gather x2, waiting for transfers between devices, body(): piece = lax.all_gather(part, 'req', axis=0, tiled=False)  86.1 us
    psum x1, blocking collectives, body(): summed = lax.psum(onehot[:, None] * summary[None, :], ('req', 'tensor'))  64.6 us
    dot_general x2, matrix products, chunk_stats(): lax.dot_general(normed, piece, (((1,), (1,)), ((), ())), preferred_elemen...  30.9 us
    all_gather x1, waiting for transfers between devices, body(): stacked = lax.all_gather(packed, 'tensor', axis=0, tiled=False)  28.3 us
    reduce_sum x1, other arithmetic, chunk_stats(): total = jnp.sum(expo, axis=1)  18.8 us
    all_gather x1, blocking collectives, body(): everyone = lax.all_gather(jnp.stack(mine), 'tensor', axis=0, tiled=False)  12.2 us
  transfers between devices with their start and end apart: 3, of which 3 were waited for; matrix products, arithmetic and copies ran while one was open for 10% of the time, Pallas kernels for 0%

commit v1 on v0

--- a/solution.py
+++ b/solution.py
@@ -1,10 +1,11 @@
 import jax
 import jax.numpy as jnp
 from jax import lax
-from jax.sharding import PartitionSpec as P
+from jax.sharding import Mesh, PartitionSpec as P
 from jax.experimental.layout import Layout, with_layout_constraint
 
 PROMPTS = 4
+REQ = ("y", "z", "c")
 NEG = -1e30
 
 eps = 1e-06
@@ -33,15 +34,21 @@
 
 def body(hidden, gain, head, token_ids, lengths, prompt_of):
     rows, part_width = hidden.shape
-    splits = lax.axis_size("tensor")
-    column_index = lax.axis_index("tensor")
-    req_count = lax.axis_size("req")
+    splits = lax.axis_size("x")
+    column_index = lax.axis_index("x")
+    req_count = lax.axis_size(REQ)
     shard_cols = head.shape[1]
     width = part_width * splits
 
     extra = jnp.zeros((8, part_width), hidden.dtype).at[0].set(gain)
     packed = jnp.concatenate([hidden, extra], axis=0)
-    stacked = lax.all_gather(packed, "tensor", axis=0, tiled=False)
+    shift = lambda x, d: lax.ppermute(x, "x", [(i, (i + d) % splits) for i in range(splits)])
+    from_left = shift(packed, 1)
+    from_right = shift(packed, -1)
+    from_far = shift(from_left, 1)
+    stacked = jnp.stack([packed, from_right, from_far, from_left])
+    order = (jnp.arange(splits, dtype=jnp.int32) - column_index) % splits
+    stacked = jnp.take(stacked, order, axis=0)
     gathered = jnp.transpose(stacked, (1, 0, 2)).reshape(rows + 8, width)
     widened = gathered[:rows].astype(jnp.float32)
     gain_full = gathered[rows].astype(jnp.float32)
@@ -56,7 +63,7 @@
         if hi - lo < chunk:
             part = jnp.concatenate([part, jnp.zeros((chunk - (hi - lo), part.shape[1]), part.dtype)], axis=0)
         part = with_layout_constraint(part, Layout(major_to_minor=(0, 1)))
-        piece = lax.all_gather(part, "req", axis=0, tiled=False)
+        piece = lax.all_gather(part, REQ, axis=0, tiled=False)
         piece = with_layout_constraint(piece, Layout(major_to_minor=(0, 1, 2)))
         piece = piece.reshape(req_count * chunk, piece.shape[2])
         g = jnp.arange(req_count * chunk, dtype=jnp.int32)
@@ -67,7 +74,7 @@
         stats.append(chunk_stats(normed, piece, vocab_ids, valid, token_ids))
     mine = merge(stats)
 
-    everyone = lax.all_gather(jnp.stack(mine), "tensor", axis=0, tiled=False)
+    everyone = lax.all_gather(jnp.stack(mine), "x", axis=0, tiled=False)
     top, total, moment, picked = merge([tuple(everyone[k, j] for j in range(4)) for k in range(splits)])
 
     positions = jnp.arange(rows, dtype=jnp.int32)
@@ -82,19 +89,23 @@
     own_entropy = lax.dynamic_slice_in_dim(entropy, column_index * share, share)
     count = jnp.where(column_index == 0, lengths[0], 0).astype(jnp.float32)
     summary = jnp.stack([jnp.sum(own_entropy), jnp.sum(own_logprob), count])
-    summed = lax.psum(onehot[:, None] * summary[None, :], ("req", "tensor"))
+    summed = onehot[:, None] * summary[None, :]
+    for name in ("c", "z", "y", "x"):
+        summed = lax.psum(summed, name)
     prompt_stats = summed[:, :2] / jnp.maximum(summed[:, 2:3], 1.0)
     return (own_logprob, own_entropy, prompt_stats)
 
 
 def solution(mesh):
+    req_axes = mesh.devices.shape[0] // 8
+    fine = Mesh(mesh.devices.reshape(req_axes, 4, 2, mesh.devices.shape[1]), ("y", "z", "c", "x"))
     in_specs = (
-        P("req", "tensor"),
-        P("tensor"),
-        P(None, ("req", "tensor")),
-        P("req"),
-        P("req"),
-        P("req"),
+        P(REQ, "x"),
+        P("x"),
+        P(None, REQ + ("x",)),
+        P(REQ),
+        P(REQ),
+        P(REQ),
     )
-    out_specs = (P(("req", "tensor")), P(("req", "tensor")), P())
-    return jax.shard_map(body, mesh=mesh, in_specs=in_specs, out_specs=out_specs, check_vma=False)
+    out_specs = (P(REQ + ("x",)), P(REQ + ("x",)), P())
+    return jax.shard_map(body, mesh=fine, in_specs=in_specs, out_specs=out_specs, check_vma=False)

time: 274 us -> 209 us (0.76)
  waiting for transfers between devices: 114 us -> 77.1 us
  blocking collectives: 76.8 us -> 43.7 us
  starting transfers between devices: 0.12 us -> 3.86 us
    all_gather x3 -> x2, waiting for transfers between devices: 114 us -> 53.3 us  [body(): piece = lax.all_gather(part, REQ, axis=0, tiled=False)]
    psum x1 -> x4, blocking collectives: 64.6 us -> 31.5 us  [body(): summed = lax.psum(summed, name)]
    ppermute x0 -> x3, waiting for transfers between devices: none -> 23.8 us  [body(): lax.ppermute(x, 'x', [(i, (i + d) % splits) for i in range(splits)])]
    ppermute x0 -> x3, starting transfers between devices: none -> 3.78 us  [body(): lax.ppermute(x, 'x', [(i, (i + d) % splits) for i in range(splits)])]
  transfers between devices with their start and end apart: 3 -> 5, of which waited for: 3 -> 4; matrix products, arithmetic and copies ran while one was open for 10% -> 14% of each run, Pallas kernels for 0% -> 0%
where the time goes in v1:
time: 209 us; the launch traced here: 208 us
  waiting for transfers between devices  77.1 us (37%)
  blocking collectives  43.7 us (21%)
  matrix products  30.9 us (15%)
  other arithmetic  28.1 us (13%)
  between operations  15.5 us (7%)
  local copies, waits for them, and re-layouts  9.06 us (4%)
  starting transfers between devices  3.86 us (2%)
    all_gather x2, waiting for transfers between devices, body(): piece = lax.all_gather(part, REQ, axis=0, tiled=False)  53.3 us
    psum x4, blocking collectives, body(): summed = lax.psum(summed, name)  31.5 us
    dot_general x2, matrix products, chunk_stats(): lax.dot_general(normed, piece, (((1,), (1,)), ((), ())), preferred_elemen...  30.9 us
    ppermute x3, waiting for transfers between devices, body(): lax.ppermute(x, 'x', [(i, (i + d) % splits) for i in range(splits)])  23.8 us
    reduce_sum x1, other arithmetic, chunk_stats(): total = jnp.sum(expo, axis=1)  19.1 us
    all_gather x1, blocking collectives, body(): everyone = lax.all_gather(jnp.stack(mine), 'x', axis=0, tiled=False)  12.2 us
  transfers between devices with their start and end apart: 5, of which 4 were waited for; matrix products, arithmetic and copies ran while one was open for 14% of the time, Pallas kernels for 0%

profile of v1, /device:TPU:0, one launch (start us, length us, event | category | flops | bytes accessed | tf_op | source)
XLA Modules:
  0.0 208.2 jit_solution(265337625337042231)
XLA Ops:
  7.2 0.0 all-gather.9.cloned.1.call-start
  7.2 1.0 slice.85
  8.2 0.2 copy.24
  8.4 0.8 concatenate.9
  9.1 0.0 all-gather.9.cloned.1.call-update
  9.1 0.0 all-gather.7.cloned.1.call-start
  9.2 1.0 slice.84
  10.2 0.9 copy.23
  11.1 0.0 all-gather.7.cloned.1.call-update
  11.1 0.7 reshape.241
  11.7 1.1 fusion.32
  12.9 1.7 collective-permute-start.1
  14.5 1.6 collective-permute-start
  17.5 10.3 %collective-permute-done.1 = bf16[1032,256]{1,0:T(8,128)(2,1)S(1)} collective-permute-done((bf16[1032,256]{1,0:T(8,128)(2,1)S(1)}, bf16[1032,256]{1,0:T(8,128)(2,1)S(1)}, u32[]{:S(2)}, u32[]{:S(2)}) %collective-permute-start.1) | collective-permute-done | bytes 528416 | tf_op jit(solution)/shard_map/ppermute | solution.py:45
  27.8 0.5 collective-permute-start.2
  28.3 0.0 collective-permute-done
  28.3 0.0 copy-start.1
  28.3 13.5 %collective-permute-done.2 = bf16[1032,256]{1,0:T(8,128)(2,1)S(1)} collective-permute-done((bf16[1032,256]{1,0:T(8,128)(2,1)S(1)}, bf16[1032,256]{1,0:T(8,128)(2,1)S(1)}, u32[]{:S(2)}, u32[]{:S(2)}) %collective-permute-start.2) | collective-permute-done | bytes 528416 | tf_op jit(solution)/shard_map/ppermute | solution.py:45
  41.8 0.0 copy-done.1
  41.8 1.3 pad_maximum_fusion
  43.1 2.1 gather_fusion
  45.2 1.9 select_bitcast_fusion
  47.1 0.5 fusion.2
  47.6 0.5 fusion.4
  48.1 2.5 %copy.19 = bf16[1024,4,256]{0,2,1:T(8,128)(2,1)} copy(bf16[1024,4,256]{2,0,1:T(8,128)(2,1)S(1)} %fusion.4) | data formatting | bytes 4194304 | tf_op jit(solution)/shard_map/convert_element_type | solution.py:56
  50.7 14.9 %all-gather.9.cloned.1.call-done = bf16[4096,1024]{1,0:T(8,128)(2,1)} async-done(((bf16[128,1024]{1,0:T(8,128)(2,1)}), bf16[4096,1024]{1,0:T(8,128)(2,1)}) %all-gather.9.cloned.1.call-update) | async-done | bytes 8388624 | tf_op jit(solution)/shard_map/all_gather | solution.py:66
  65.6 0.0 copy-start
  65.6 16.3 %select_reduce_fusion.2 = (f32[1024]{0:T(1024)S(1)}, f32[1024,4096]{1,0:T(8,128)}) fusion(pred[4096]{0:T(1024)(128)(4,1)S(1)} %fusion.22, bf16[1024,1024]{0,1:T(8,128)(2,1)} %bitcast.72, bf16[4096,1024]{1,0:T(8,128)(2,1)} %all-gather.9.cloned.1.call-done), kind=kOutput, calls=%fused_computation.9 | convolution fusion | flops 8598322176 | bytes 27271168 | tf_op jit(solution)/shard_map/dot_general | solution.py:15
  82.0 0.0 copy-start.2
  82.0 38.3 %all-gather.7.cloned.1.call-done = bf16[4096,1024]{1,0:T(8,128)(2,1)} async-done(((bf16[128,1024]{1,0:T(8,128)(2,1)}), bf16[4096,1024]{1,0:T(8,128)(2,1)}) %all-gather.7.cloned.1.call-update) | async-done | bytes 8388624 | tf_op jit(solution)/shard_map/all_gather | solution.py:66
  120.3 0.0 copy-done
  120.3 14.6 %select_reduce_fusion.3 = (f32[1024]{0:T(1024)S(1)}, f32[1024,4096]{1,0:T(8,128)}) fusion(pred[4096]{0:T(1024)(128)(4,1)S(1)} %fusion.21, bf16[1024,1024]{0,1:T(8,128)(2,1)S(1)} %bitcast.73, bf16[4096,1024]{1,0:T(8,128)(2,1)} %all-gather.7.cloned.1.call-done), kind=kOutput, calls=%fused_computation.10 | convolution fusion | flops 8598322176 | bytes 27271168 | tf_op jit(solution)/shard_map/dot_general | solution.py:15
  134.9 0.0 copy-done.2
  134.9 19.1 %fusion = (f32[1024]{0:T(1024)S(1)}, f32[1024]{0:T(1024)S(1)}, f32[1024]{0:T(1024)S(1)}, f32[1024]{0:T(1024)S(1)}, f32[1024]{0:T(1024)S(1)}, /*index=5*/f32[1024]{0:T(1024)S(1)}) fusion(f32[1024,4096]{1,0:T(8,128)} %get-tuple-element.50, f32[1024]{0:T(1024)S(1)} %get-tuple-element.49, pred[4096]{0:T(1024)(128)(4,1)S(1)} %fusion.22, s32[1024]{0:T(1024)S(1)} %copy-done.2, ...), kind=kLoop, calls=%fused_computation.6 | loop fusion | flops 67102720 | bytes 33632256 | tf_op jit(solution)/shard_map/reduce_sum | solution.py:19
  154.2 12.2 %all-gather.3 = f32[4,4,1024]{2,1,0:T(4,128)S(1)} all-gather(f32[1,4,1024]{2,1,0:T(4,128)S(1)} %maximum_bitcast_fusion), channel_id=4, replica_groups=mesh['y'=4,'z'=4,'c'=2,'x'=4] {'x'}, dimensions={0}, use_global_device_ids=true | all-gather | bytes 81920 | tf_op jit(solution)/shard_map/all_gather | solution.py:77
  166.4 0.1 fusion.17
  166.5 1.3 fusion.33
  167.8 1.4 pad_maximum_fusion.1
  169.2 0.1 broadcast_multiply_fusion
  169.3 2.4 %psum.28 = f32[4,3]{0,1:T(4,128)S(1)} all-reduce(f32[4,3]{0,1:T(4,128)S(1)} %broadcast_multiply_fusion), channel_id=1, replica_groups=mesh['y'=4,'z'=4,'c'=2,'x'=4] {'c'}, use_global_device_ids=true, to_apply=%region_15.16 | all-reduce | flops 12 | bytes 96 | tf_op jit(solution)/shard_map/psum | solution.py:94
  171.7 10.3 %psum.29 = f32[4,3]{0,1:T(4,128)S(1)} all-reduce(f32[4,3]{0,1:T(4,128)S(1)} %psum.28), channel_id=1, replica_groups=mesh['y'=4,'z'=4,'c'=2,'x'=4] {'z'}, use_global_device_ids=true, to_apply=%region_16.17 | all-reduce | flops 12 | bytes 96 | tf_op jit(solution)/shard_map/psum | solution.py:94
  182.0 8.6 %psum.30 = f32[4,3]{0,1:T(4,128)S(1)} all-reduce(f32[4,3]{0,1:T(4,128)S(1)} %psum.29), channel_id=1, replica_groups=mesh['y'=4,'z'=4,'c'=2,'x'=4] {'y'}, use_global_device_ids=true, to_apply=%region_17.18 | all-reduce | flops 12 | bytes 96 | tf_op jit(solution)/shard_map/psum | solution.py:94
  190.7 10.1 %psum.31 = f32[4,3]{0,1:T(4,128)S(1)} all-reduce(f32[4,3]{0,1:T(4,128)S(1)} %psum.30), channel_id=1, replica_groups=mesh['y'=4,'z'=4,'c'=2,'x'=4] {'x'}, use_global_device_ids=true, to_apply=%region_18.19 | all-reduce | flops 12 | bytes 96 | tf_op jit(solution)/shard_map/psum | solution.py:94
  200.8 0.6 slice_divide_fusion
  (20 shorter events, 0.2 us)
Async XLA Ops:
  7.2 58.5 %all-gather.9.cloned.1.call-start = ((), (), s32[]{:S(2)}) async-start(), calls=%async_computation.1 | async-start | bytes 8650752 | tf_op jit(solution)/shard_map/all_gather | solution.py:66
  9.1 111.2 %all-gather.7.cloned.1.call-start = ((), (), s32[]{:S(2)}) async-start(), calls=%async_computation | async-start | bytes 8650752 | tf_op jit(solution)/shard_map/all_gather | solution.py:66
  12.9 15.0 %collective-permute-start.1 = (bf16[1032,256]{1,0:T(8,128)(2,1)S(1)}, bf16[1032,256]{1,0:T(8,128)(2,1)S(1)}, u32[]{:S(2)}, u32[]{:S(2)}) collective-permute-start(bf16[1032,256]{1,0:T(8,128)(2,1)S(1)} %get-tuple-element.30), channel_id=1, source_target_pairs={{0,1},{1,2},{2,3},{3,0},{4,5},{5,6},{6,7},{7,4},{8,9},{9,10},{10,1... | collective-permute-start | bytes 1585160 | tf_op jit(solution)/shard_map/ppermute | solution.py:45
  14.5 13.8 %collective-permute-start = (bf16[1032,256]{1,0:T(8,128)(2,1)S(1)}, bf16[1032,256]{1,0:T(8,128)(2,1)S(1)}, u32[]{:S(2)}, u32[]{:S(2)}) collective-permute-start(bf16[1032,256]{1,0:T(8,128)(2,1)S(1)} %get-tuple-element.30), channel_id=1, source_target_pairs={{0,3},{1,0},{2,1},{3,2},{4,7},{5,4},{6,5},{7,6},{8,11},{9,8},{10,9... | collective-permute-start | bytes 1585160 | tf_op jit(solution)/shard_map/ppermute | solution.py:45
  27.8 14.0 %collective-permute-start.2 = (bf16[1032,256]{1,0:T(8,128)(2,1)S(1)}, bf16[1032,256]{1,0:T(8,128)(2,1)S(1)}, u32[]{:S(2)}, u32[]{:S(2)}) collective-permute-start(bf16[1032,256]{1,0:T(8,128)(2,1)S(1)} %collective-permute-done.1), channel_id=1, source_target_pairs={{0,1},{1,2},{2,3},{3,0},{4,5},{5,6},{6,7},{7,4},{8,9},{9,10},{10,1... | collective-permute-start | bytes 1585160 | tf_op jit(solution)/shard_map/ppermute | solution.py:45
  28.3 13.5 %copy-start.1 = (bf16[1032,256]{1,0:T(8,128)(2,1)}, bf16[1032,256]{1,0:T(8,128)(2,1)S(1)}, u32[]{:S(2)}) copy-start(bf16[1032,256]{1,0:T(8,128)(2,1)S(1)} %collective-permute-done) | copy-start | bytes 1585156
  65.6 54.7 %copy-start = (bf16[1024,4,256]{0,2,1:T(8,128)(2,1)S(1)}, bf16[1024,4,256]{0,2,1:T(8,128)(2,1)}, u32[]{:S(2)}) copy-start(bf16[1024,4,256]{0,2,1:T(8,128)(2,1)} %copy.19) | copy-start | bytes 6291460
  82.0 53.0 %copy-start.2 = (s32[1024]{0:T(1024)S(1)}, s32[1024]{0:T(1024)}, u32[]{:S(2)}) copy-start(s32[1024]{0:T(1024)} %param.11) | copy-start | bytes 12292
Sparse Core Ops, SparseCore 0:
  10.2 55.3 all-gather.8
  67.9 52.3 all-gather.6

commit v2 on v1

--- a/solution.py
+++ b/solution.py
@@ -55,7 +55,7 @@
     scale = lax.rsqrt(jnp.sum(widened * widened, axis=1) / width + eps)
     normed = (widened * scale[:, None] * gain_full[None, :]).astype(jnp.bfloat16)
 
-    chunk = 128
+    chunk = 256
     bounds = [(lo, min(lo + chunk, shard_cols)) for lo in range(0, shard_cols, chunk)]
     stats = []
     for lo, hi in bounds:
@@ -87,10 +87,9 @@
     share = rows // splits
     own_logprob = lax.dynamic_slice_in_dim(logprob, column_index * share, share)
     own_entropy = lax.dynamic_slice_in_dim(entropy, column_index * share, share)
-    count = jnp.where(column_index == 0, lengths[0], 0).astype(jnp.float32)
-    summary = jnp.stack([jnp.sum(own_entropy), jnp.sum(own_logprob), count])
+    summary = jnp.stack([jnp.sum(entropy), jnp.sum(logprob), lengths[0].astype(jnp.float32)])
     summed = onehot[:, None] * summary[None, :]
-    for name in ("c", "z", "y", "x"):
+    for name in REQ[::-1]:
         summed = lax.psum(summed, name)
     prompt_stats = summed[:, :2] / jnp.maximum(summed[:, 2:3], 1.0)
     return (own_logprob, own_entropy, prompt_stats)

time: 209 us -> 175 us (0.84)
  waiting for transfers between devices: 77.1 us -> 62 us
  blocking collectives: 43.7 us -> 33.5 us
  matrix products: 30.9 us -> 26.1 us
  other arithmetic: 28.1 us -> 25.1 us
    all_gather x2 -> x1, waiting for transfers between devices: 53.3 us -> 38.2 us  [body(): piece = lax.all_gather(part, REQ, axis=0, tiled=False)]
    psum x4 -> x3, blocking collectives: 31.5 us -> 21.4 us  [body(): summed = lax.psum(summed, name)]
    dot_general x2 -> x1, matrix products: 30.9 us -> 26.1 us  [chunk_stats(): lax.dot_general(normed, piece, (((1,), (1,)), ((), ())), preferred_elemen...]
  transfers between devices with their start and end apart: 5 -> 4, of which waited for: 4 -> 3; matrix products, arithmetic and copies ran while one was open for 14% -> 5% of each run, Pallas kernels for 0% -> 0%
where the time goes in v2:
time: 175 us; the launch traced here: 174 us
  waiting for transfers between devices  62 us (35%)
  blocking collectives  33.5 us (19%)
  matrix products  26.1 us (15%)
  other arithmetic  25.1 us (14%)
  between operations  15.5 us (9%)
  local copies, waits for them, and re-layouts  7.94 us (5%)
  starting transfers between devices  3.82 us (2%)
    all_gather x1, waiting for transfers between devices, body(): piece = lax.all_gather(part, REQ, axis=0, tiled=False)  38.2 us
    dot_general x1, matrix products, chunk_stats(): lax.dot_general(normed, piece, (((1,), (1,)), ((), ())), preferred_elemen...  26.1 us
    ppermute x3, waiting for transfers between devices, body(): lax.ppermute(x, 'x', [(i, (i + d) % splits) for i in range(splits)])  23.8 us
    psum x3, blocking collectives, body(): summed = lax.psum(summed, name)  21.4 us
    reduce_sum x1, other arithmetic, chunk_stats(): total = jnp.sum(expo, axis=1)  18 us
    all_gather x1, blocking collectives, body(): everyone = lax.all_gather(jnp.stack(mine), 'x', axis=0, tiled=False)  12.2 us
    ppermute x3, starting transfers between devices, body(): lax.ppermute(x, 'x', [(i, (i + d) % splits) for i in range(splits)])  3.78 us
  transfers between devices with their start and end apart: 4, of which 3 were waited for; matrix products, arithmetic and copies ran while one was open for 5% of the time, Pallas kernels for 0%

profile of v2, /device:TPU:0, one launch (start us, length us, event | category | flops | bytes accessed | tf_op | source)
XLA Modules:
  0.0 174.0 jit_solution(8851995685780477343)
XLA Ops:
  7.2 0.0 copy-start.3
  7.2 0.0 copy-start.1
  7.2 0.0 all-gather.5.cloned.1.call-start
  7.2 1.3 copy.16
  8.5 0.8 concatenate.9
  9.4 0.0 all-gather.5.cloned.1.call-update
  9.4 0.0 copy-done.3
  9.4 0.0 copy-done.1
  9.4 0.1 fusion.26
  9.5 1.7 collective-permute-start.1
  11.2 1.6 collective-permute-start
  14.1 10.3 %collective-permute-done.1 = bf16[1032,256]{1,0:T(8,128)(2,1)S(1)} collective-permute-done((bf16[1032,256]{1,0:T(8,128)(2,1)S(1)}, bf16[1032,256]{1,0:T(8,128)(2,1)S(1)}, u32[]{:S(2)}, u32[]{:S(2)}) %collective-permute-start.1) | collective-permute-done | bytes 528416 | tf_op jit(solution)/shard_map/ppermute | solution.py:45
  24.5 0.5 collective-permute-start.2
  25.0 0.0 collective-permute-done
  25.0 0.0 copy-start
  25.0 13.5 %collective-permute-done.2 = bf16[1032,256]{1,0:T(8,128)(2,1)S(1)} collective-permute-done((bf16[1032,256]{1,0:T(8,128)(2,1)S(1)}, bf16[1032,256]{1,0:T(8,128)(2,1)S(1)}, u32[]{:S(2)}, u32[]{:S(2)}) %collective-permute-start.2) | collective-permute-done | bytes 528416 | tf_op jit(solution)/shard_map/ppermute | solution.py:45
  38.5 0.0 copy-done
  38.5 1.3 pad_maximum_fusion
  39.8 2.0 %gather_fusion = bf16[4,1032,256]{2,1,0:T(8,128)(2,1)} fusion(bf16[4,1032,256]{2,1,0:T(8,128)(2,1)S(1)} %pad_maximum_fusion, s32[1024]{0:T(1024)S(1)} %pad_clamp_fusion), kind=kCustom, calls=%fused_computation | custom fusion | bytes 4227088 | tf_op jit(solution)/shard_map/jit(_take)/gather | solution.py:51
  41.8 1.9 %select_bitcast_fusion = bf16[1032,4,256]{2,0,1:T(8,128)(2,1)S(1)} fusion(bf16[4,1032,256]{2,1,0:T(8,128)(2,1)} %gather_fusion, pred[4]{0:T(512)(128)(4,1)S(1)} %compare_and_fusion), kind=kLoop, calls=%fused_computation.12 | loop fusion | flops 1056768 | bytes 4227076 | tf_op jit(solution)/shard_map/jit(_take)/select_n | solution.py:51
  43.7 0.5 fusion.1
  44.2 0.5 fusion.3
  44.8 2.5 %copy.15 = bf16[1024,4,256]{0,2,1:T(8,128)(2,1)} copy(bf16[1024,4,256]{2,0,1:T(8,128)(2,1)S(1)} %fusion.3) | data formatting | bytes 4194304 | tf_op jit(solution)/shard_map/convert_element_type | solution.py:56
  47.2 38.2 %all-gather.5.cloned.1.call-done = bf16[8192,1024]{1,0:T(8,128)(2,1)} async-done(((bf16[256,1024]{1,0:T(8,128)(2,1)}), bf16[8192,1024]{1,0:T(8,128)(2,1)}) %all-gather.5.cloned.1.call-update) | async-done | bytes 16777232 | tf_op jit(solution)/shard_map/all_gather | solution.py:66
  85.5 0.0 copy-start.2
  85.5 26.1 %select_reduce_fusion.1 = (f32[1024]{0:T(1024)S(1)}, f32[1024,8192]{1,0:T(8,128)}) fusion(pred[8192]{0:T(1024)(128)(4,1)S(1)} %fusion.14, bf16[1024,1024]{0,1:T(8,128)(2,1)} %bitcast.61, bf16[8192,1024]{1,0:T(8,128)(2,1)} %all-gather.5.cloned.1.call-done), kind=kOutput, calls=%fused_computation.5 | convolution fusion | flops 17196646400 | bytes 52441088 | tf_op jit(solution)/shard_map/dot_general | solution.py:15
  111.5 0.0 copy-done.2
  111.5 18.0 %fusion = (f32[1024]{0:T(1024)S(1)}, f32[1024]{0:T(1024)S(1)}, f32[1024]{0:T(1024)S(1)}) fusion(f32[1024,8192]{1,0:T(8,128)} %get-tuple-element.44, f32[1024]{0:T(1024)S(1)} %get-tuple-element.43, pred[8192]{0:T(1024)(128)(4,1)S(1)} %fusion.14, s32[1024]{0:T(1024)S(1)} %copy-done.2, s32[8192]{0:T(1024)S(1)} %fusion.11), kind=kLoop, calls=%fused_computation.4 | loop fusion | flops 67105792 | bytes 33615872 | tf_op jit(solution)/shard_map/reduce_sum | solution.py:19
  129.6 12.2 %all-gather.2 = f32[4,4,1024]{2,1,0:T(4,128)S(1)} all-gather(f32[1,4,1024]{2,1,0:T(4,128)S(1)} %maximum_bitcast_fusion), channel_id=3, replica_groups=mesh['y'=4,'z'=4,'c'=2,'x'=4] {'x'}, dimensions={0}, use_global_device_ids=true | all-gather | bytes 81920 | tf_op jit(solution)/shard_map/all_gather | solution.py:77
  141.8 0.1 fusion.19
  141.9 0.6 fusion.27
  142.5 1.4 pad_maximum_fusion.1
  143.9 0.1 broadcast_multiply_fusion
  143.9 2.4 %psum.21 = f32[4,3]{0,1:T(4,128)S(1)} all-reduce(f32[4,3]{0,1:T(4,128)S(1)} %broadcast_multiply_fusion), channel_id=1, replica_groups=mesh['y'=4,'z'=4,'c'=2,'x'=4] {'c'}, use_global_device_ids=true, to_apply=%region_9.10 | all-reduce | flops 12 | bytes 96 | tf_op jit(solution)/shard_map/psum | solution.py:93
  146.4 10.1 %psum.22 = f32[4,3]{0,1:T(4,128)S(1)} all-reduce(f32[4,3]{0,1:T(4,128)S(1)} %psum.21), channel_id=1, replica_groups=mesh['y'=4,'z'=4,'c'=2,'x'=4] {'z'}, use_global_device_ids=true, to_apply=%region_10.11 | all-reduce | flops 12 | bytes 96 | tf_op jit(solution)/shard_map/psum | solution.py:93
  156.5 8.8 %psum.23 = f32[4,3]{0,1:T(4,128)S(1)} all-reduce(f32[4,3]{0,1:T(4,128)S(1)} %psum.22), channel_id=1, replica_groups=mesh['y'=4,'z'=4,'c'=2,'x'=4] {'y'}, use_global_device_ids=true, to_apply=%region_11.12 | all-reduce | flops 12 | bytes 96 | tf_op jit(solution)/shard_map/psum | solution.py:93
  165.3 0.6 slice_divide_fusion
  165.9 0.6 dynamic_slice.7
  166.5 0.6 dynamic_slice.6
  (15 shorter events, 0.2 us)
Async XLA Ops:
  7.2 2.2 %copy-start.3 = (bf16[256]{0:T(256)(128)(2,1)S(1)}, bf16[256]{0:T(256)(128)(2,1)}, u32[]{:S(2)}) copy-start(bf16[256]{0:T(256)(128)(2,1)} %param.9) | copy-start | bytes 1540
  7.2 2.2 %copy-start.1 = (bf16[1024,256]{1,0:T(8,128)(2,1)S(1)}, bf16[1024,256]{1,0:T(8,128)(2,1)}, u32[]{:S(2)}) copy-start(bf16[1024,256]{1,0:T(8,128)(2,1)} %param.8) | copy-start | bytes 1572868
  7.2 78.3 %all-gather.5.cloned.1.call-start = ((), (), s32[]{:S(2)}) async-start(), calls=%async_computation | async-start | bytes 17301504 | tf_op jit(solution)/shard_map/all_gather | solution.py:66
  9.5 15.0 %collective-permute-start.1 = (bf16[1032,256]{1,0:T(8,128)(2,1)S(1)}, bf16[1032,256]{1,0:T(8,128)(2,1)S(1)}, u32[]{:S(2)}, u32[]{:S(2)}) collective-permute-start(bf16[1032,256]{1,0:T(8,128)(2,1)S(1)} %get-tuple-element.25), channel_id=1, source_target_pairs={{0,1},{1,2},{2,3},{3,0},{4,5},{5,6},{6,7},{7,4},{8,9},{9,10},{10,1... | collective-permute-start | bytes 1585160 | tf_op jit(solution)/shard_map/ppermute | solution.py:45
  11.2 13.8 %collective-permute-start = (bf16[1032,256]{1,0:T(8,128)(2,1)S(1)}, bf16[1032,256]{1,0:T(8,128)(2,1)S(1)}, u32[]{:S(2)}, u32[]{:S(2)}) collective-permute-start(bf16[1032,256]{1,0:T(8,128)(2,1)S(1)} %get-tuple-element.25), channel_id=1, source_target_pairs={{0,3},{1,0},{2,1},{3,2},{4,7},{5,4},{6,5},{7,6},{8,11},{9,8},{10,9... | collective-permute-start | bytes 1585160 | tf_op jit(solution)/shard_map/ppermute | solution.py:45
  24.5 14.0 %collective-permute-start.2 = (bf16[1032,256]{1,0:T(8,128)(2,1)S(1)}, bf16[1032,256]{1,0:T(8,128)(2,1)S(1)}, u32[]{:S(2)}, u32[]{:S(2)}) collective-permute-start(bf16[1032,256]{1,0:T(8,128)(2,1)S(1)} %collective-permute-done.1), channel_id=1, source_target_pairs={{0,1},{1,2},{2,3},{3,0},{4,5},{5,6},{6,7},{7,4},{8,9},{9,10},{10,1... | collective-permute-start | bytes 1585160 | tf_op jit(solution)/shard_map/ppermute | solution.py:45
  25.0 13.5 %copy-start = (bf16[1032,256]{1,0:T(8,128)(2,1)}, bf16[1032,256]{1,0:T(8,128)(2,1)S(1)}, u32[]{:S(2)}) copy-start(bf16[1032,256]{1,0:T(8,128)(2,1)S(1)} %collective-permute-done) | copy-start | bytes 1585156
  85.5 26.1 %copy-start.2 = (s32[1024]{0:T(1024)S(1)}, s32[1024]{0:T(1024)}, u32[]{:S(2)}) copy-start(s32[1024]{0:T(1024)} %param.11) | copy-start | bytes 12292
Sparse Core Ops, SparseCore 0:
  10.3 75.1 all-gather.4

commit v3 on v2

--- a/solution.py
+++ b/solution.py
@@ -36,7 +36,6 @@
     rows, part_width = hidden.shape
     splits = lax.axis_size("x")
     column_index = lax.axis_index("x")
-    req_count = lax.axis_size(REQ)
     shard_cols = head.shape[1]
     width = part_width * splits
 
@@ -56,22 +55,27 @@
     normed = (widened * scale[:, None] * gain_full[None, :]).astype(jnp.bfloat16)
 
     chunk = 256
-    bounds = [(lo, min(lo + chunk, shard_cols)) for lo in range(0, shard_cols, chunk)]
-    stats = []
-    for lo, hi in bounds:
-        part = head[:, lo:hi].T
-        if hi - lo < chunk:
-            part = jnp.concatenate([part, jnp.zeros((chunk - (hi - lo), part.shape[1]), part.dtype)], axis=0)
-        part = with_layout_constraint(part, Layout(major_to_minor=(0, 1)))
-        piece = lax.all_gather(part, REQ, axis=0, tiled=False)
-        piece = with_layout_constraint(piece, Layout(major_to_minor=(0, 1, 2)))
-        piece = piece.reshape(req_count * chunk, piece.shape[2])
-        g = jnp.arange(req_count * chunk, dtype=jnp.int32)
-        owner = g // chunk
-        offset = lo + g % chunk
-        valid = offset < hi
-        vocab_ids = jnp.where(valid, (owner * splits + column_index) * shard_cols + offset, -1)
-        stats.append(chunk_stats(normed, piece, vocab_ids, valid, token_ids))
+    part = head.T
+    part = jnp.concatenate([part, jnp.zeros((chunk - shard_cols, part.shape[1]), part.dtype)], axis=0)
+    part = with_layout_constraint(part, Layout(major_to_minor=(0, 1)))
+    plane = lax.all_gather(part, ("y", "z"), axis=0, tiled=False)
+    plane = with_layout_constraint(plane, Layout(major_to_minor=(0, 1, 2)))
+    core = lax.axis_index("c")
+    cores = lax.axis_size("c")
+    blocks = plane.shape[0]
+    g = jnp.arange(blocks * chunk, dtype=jnp.int32)
+    offset = g % chunk
+    valid = offset < shard_cols
+
+    def ids_for(c):
+        owner = (g // chunk) * cores + c
+        return jnp.where(valid, (owner * splits + column_index) * shard_cols + offset, -1)
+
+    other = lax.ppermute(plane, "c", [(i, (i + 1) % cores) for i in range(cores)])
+    first = chunk_stats(normed, plane.reshape(blocks * chunk, -1), ids_for(core), valid, token_ids)
+    first, normed_later = lax.optimization_barrier((first, normed))
+    second = chunk_stats(normed_later, other.reshape(blocks * chunk, -1), ids_for((core + 1) % cores), valid, token_ids)
+    stats = [first, second]
     mine = merge(stats)
 
     everyone = lax.all_gather(jnp.stack(mine), "x", axis=0, tiled=False)

time: 175 us -> 232 us (1.33)
  waiting for transfers between devices: 62 us -> 99.8 us
  other arithmetic: 25.1 us -> 34 us
  local copies, waits for them, and re-layouts: 7.94 us -> 15.5 us
  matrix products: 26.1 us -> 29.5 us
    all_gather x1, waiting for transfers between devices: 38.2 us -> 74.3 us  [body(): plane = lax.all_gather(part, ('y', 'z'), axis=0, tiled=False)]
    reduce_sum x0 -> x3, other arithmetic: none -> 9.59 us  [the longest x1 9.54 us: chunk_stats(): moment = jnp.sum(expo * logits, axis=1)]
    reduce_sum x1, other arithmetic: 18 us -> 9.92 us  [chunk_stats(): total = jnp.sum(expo, axis=1)]
    convert_element_type x0 -> x1, local copies, waits for them, and re-layouts: none -> 5.41 us  [body(): widened = gathered[:rows].astype(jnp.float32)]
    convert_element_type x1 -> x2, other arithmetic: 0.55 us -> 4.59 us  [body(): (widened * scale[:, None] * gain_full[None, :]).astype(jnp.bfloat16)]
    dot_general x1 -> x2, matrix products: 26.1 us -> 29.5 us  [chunk_stats(): lax.dot_general(normed, piece, (((1,), (1,)), ((), ())), preferred_elemen...]
  transfers between devices with their start and end apart: 4 -> 5, of which waited for: 3 -> 3; matrix products, arithmetic and copies ran while one was open for 5% -> 21% of each run, Pallas kernels for 0% -> 0%
where the time goes in v3:
time: 232 us; the launch traced here: 231 us
  waiting for transfers between devices  99.8 us (43%)
  other arithmetic  34 us (15%)
  blocking collectives  33.3 us (14%)
  matrix products  29.5 us (13%)
  local copies, waits for them, and re-layouts  15.5 us (7%)
  between operations  15.5 us (7%)
  starting transfers between devices  3.6 us (2%)
    all_gather x1, waiting for transfers between devices, body(): plane = lax.all_gather(part, ('y', 'z'), axis=0, tiled=False)  74.3 us
    dot_general x2, matrix products, chunk_stats(): lax.dot_general(normed, piece, (((1,), (1,)), ((), ())), preferred_elemen...  29.5 us
    ppermute x3, waiting for transfers between devices, body(): lax.ppermute(x, 'x', [(i, (i + d) % splits) for i in range(splits)])  25.5 us
    psum x3, blocking collectives, body(): summed = lax.psum(summed, name)  21.4 us
    all_gather x1, blocking collectives, body(): everyone = lax.all_gather(jnp.stack(mine), 'x', axis=0, tiled=False)  11.9 us
    reduce_sum x1, other arithmetic, chunk_stats(): total = jnp.sum(expo, axis=1)  9.92 us
    reduce_sum x1, other arithmetic, chunk_stats(): moment = jnp.sum(expo * logits, axis=1)  9.54 us
    convert_element_type x1, local copies, waits for them, and re-layouts, body(): widened = gathered[:rows].astype(jnp.float32)  5.41 us
  transfers between devices with their start and end apart: 5, of which 3 were waited for; matrix products, arithmetic and copies ran while one was open for 21% of the time, Pallas kernels for 0%

profile of v3, /device:TPU:0, one launch (start us, length us, event | category | flops | bytes accessed | tf_op | source)
XLA Modules:
  0.0 231.2 jit_solution(1634605536486382630)
XLA Ops:
  7.2 0.0 all-gather.5.cloned.1.call-start
  7.2 1.2 copy.18
  8.5 0.8 concatenate.9
  9.3 0.0 all-gather.5.cloned.1.call-update
  9.3 74.3 %all-gather.5.cloned.1.call-done = bf16[4096,1024]{1,0:T(8,128)(2,1)} async-done(((bf16[256,1024]{1,0:T(8,128)(2,1)}), bf16[4096,1024]{1,0:T(8,128)(2,1)}) %all-gather.5.cloned.1.call-update) | async-done | bytes 8388624 | tf_op jit(solution)/shard_map/all_gather | solution.py:61
  83.6 0.0 collective-permute-start.3
  83.6 0.7 reshape.221
  84.2 1.1 fusion.35
  85.3 1.5 collective-permute-start.1
  86.9 1.8 collective-permute-start
  90.0 11.1 %collective-permute-done.1 = bf16[1032,256]{1,0:T(8,128)(2,1)S(1)} collective-permute-done((bf16[1032,256]{1,0:T(8,128)(2,1)S(1)}, bf16[1032,256]{1,0:T(8,128)(2,1)S(1)}, u32[]{:S(2)}, u32[]{:S(2)}) %collective-permute-start.1) | collective-permute-done | bytes 528416 | tf_op jit(solution)/shard_map/ppermute | solution.py:44
  101.1 0.3 collective-permute-start.2
  101.4 0.0 collective-permute-done
  101.4 0.0 copy-start.1
  101.4 14.4 %collective-permute-done.2 = bf16[1032,256]{1,0:T(8,128)(2,1)S(1)} collective-permute-done((bf16[1032,256]{1,0:T(8,128)(2,1)S(1)}, bf16[1032,256]{1,0:T(8,128)(2,1)S(1)}, u32[]{:S(2)}, u32[]{:S(2)}) %collective-permute-start.2) | collective-permute-done | bytes 528416 | tf_op jit(solution)/shard_map/ppermute | solution.py:44
  115.8 0.0 copy-done.1
  115.8 1.3 pad_maximum_fusion
  117.1 2.0 gather_fusion
  119.2 1.9 select_bitcast_fusion
  121.1 0.5 multiply_reduce_fusion.2
  121.6 1.8 multiply_convert_fusion
  123.4 4.0 %copy.17 = bf16[1024,4,256]{0,2,1:T(8,128)(2,1)} copy(bf16[1024,4,256]{2,0,1:T(8,128)(2,1)} %multiply_convert_fusion) | data formatting | bytes 4194304 | tf_op jit(solution)/shard_map/convert_element_type | solution.py:55
  127.4 2.3 slice_convert_fusion
  129.6 5.4 %copy.19 = f32[1024,4,256]{0,2,1:T(8,128)} copy(f32[1024,4,256]{2,0,1:T(8,128)} %slice_convert_fusion) | data formatting | bytes 8388608 | tf_op jit(solution)/shard_map/convert_element_type | solution.py:52
  135.1 0.0 copy-start
  135.1 2.8 %fusion.3 = bf16[1024,1024]{0,1:T(8,128)(2,1)S(1)} fusion(f32[1024,4,256]{0,2,1:T(8,128)} %copy.19, f32[1024]{0:T(1024)S(1)} %bitcast.82, f32[1024]{0:T(1024)S(1)} %add_rsqrt_fusion), kind=kLoop, calls=%fused_computation.13 | loop fusion | flops 3145728 | bytes 6299648 | tf_op jit(solution)/shard_map/convert_element_type | solution.py:55
  137.8 0.1 copy-done
  137.9 0.0 copy-start.2
  137.9 14.7 %select_reduce_fusion.3 = (f32[1024]{0:T(1024)S(1)}, f32[1024,4096]{1,0:T(8,128)}) fusion(pred[4096]{0:T(1024)(128)(4,1)S(1)} %fusion.25, bf16[1024,1024]{0,1:T(8,128)(2,1)S(1)} %bitcast.77, bf16[4096,1024]{1,0:T(8,128)(2,1)} %all-gather.5.cloned.1.call-done), kind=kOutput, calls=%fused_computation.10 | convolution fusion | flops 8598322176 | bytes 27271168 | tf_op jit(solution)/shard_map/dot_general | solution.py:15
  152.6 0.0 copy-done.2
  152.6 9.5 %multiply_reduce_fusion.1 = (f32[1024]{0:T(1024)S(1)}, f32[1024]{0:T(1024)S(1)}, f32[1024]{0:T(1024)S(1)}) fusion(f32[1024,4096]{1,0:T(8,128)} %get-tuple-element.57, f32[1024]{0:T(1024)S(1)} %get-tuple-element.20, pred[4096]{0:T(1024)(128)(4,1)S(1)} %fusion.25, s32[1024]{0:T(1024)S(1)} %copy-done.2, s32[4096]{0:T(1024)S(1)} %fusion.14), kind=kLoop, calls=%fused_computation.6 | loop fusion | flops 33551360 | bytes 16818176 | tf_op jit(solution)/shard_map/reduce_sum | solution.py:20
  162.1 0.0 collective-permute-done.3
  162.1 14.8 %select_reduce_fusion.2 = (f32[1024]{0:T(1024)S(1)}, f32[1024,4096]{1,0:T(8,128)}) fusion(pred[4096]{0:T(1024)(128)(4,1)S(1)} %fusion.25, bf16[1024,1024]{0,1:T(8,128)(2,1)S(1)} %fusion.3, bf16[4096,1024]{1,0:T(8,128)(2,1)} %bitcast.13), kind=kOutput, calls=%fused_computation.9 | convolution fusion | flops 8598322176 | bytes 27271168 | tf_op jit(solution)/shard_map/dot_general | solution.py:15
  177.0 9.9 %fusion = (f32[1024]{0:T(1024)S(1)}, f32[1024]{0:T(1024)S(1)}, f32[1024]{0:T(1024)S(1)}) fusion(f32[1024,4096]{1,0:T(8,128)} %get-tuple-element.59, f32[1024]{0:T(1024)S(1)} %get-tuple-element.58, pred[4096]{0:T(1024)(128)(4,1)S(1)} %fusion.25, s32[1024]{0:T(1024)S(1)} %copy-done.2, s32[4096]{0:T(1024)S(1)} %fusion.19), kind=kLoop, calls=%fused_computation.4 | loop fusion | flops 33551360 | bytes 16818176 | tf_op jit(solution)/shard_map/reduce_sum | solution.py:19
  187.0 11.9 %all-gather.2 = f32[4,4,1024]{2,1,0:T(4,128)S(1)} all-gather(f32[1,4,1024]{2,1,0:T(4,128)S(1)} %maximum_bitcast_fusion), channel_id=3, replica_groups=mesh['y'=4,'z'=4,'c'=2,'x'=4] {'x'}, dimensions={0}, use_global_device_ids=true | all-gather | bytes 81920 | tf_op jit(solution)/shard_map/all_gather | solution.py:81
  198.9 0.1 fusion.22
  199.0 0.6 fusion.36
  199.6 1.4 pad_maximum_fusion.1
  201.0 0.1 broadcast_multiply_fusion
  201.1 2.4 %psum.21 = f32[4,3]{0,1:T(4,128)S(1)} all-reduce(f32[4,3]{0,1:T(4,128)S(1)} %broadcast_multiply_fusion), channel_id=1, replica_groups=mesh['y'=4,'z'=4,'c'=2,'x'=4] {'c'}, use_global_device_ids=true, to_apply=%region_15.16 | all-reduce | flops 12 | bytes 96 | tf_op jit(solution)/shard_map/psum | solution.py:97
  203.5 10.4 %psum.22 = f32[4,3]{0,1:T(4,128)S(1)} all-reduce(f32[4,3]{0,1:T(4,128)S(1)} %psum.21), channel_id=1, replica_groups=mesh['y'=4,'z'=4,'c'=2,'x'=4] {'z'}, use_global_device_ids=true, to_apply=%region_16.17 | all-reduce | flops 12 | bytes 96 | tf_op jit(solution)/shard_map/psum | solution.py:97
  213.9 8.6 %psum.23 = f32[4,3]{0,1:T(4,128)S(1)} all-reduce(f32[4,3]{0,1:T(4,128)S(1)} %psum.22), channel_id=1, replica_groups=mesh['y'=4,'z'=4,'c'=2,'x'=4] {'y'}, use_global_device_ids=true, to_apply=%region_17.18 | all-reduce | flops 12 | bytes 96 | tf_op jit(solution)/shard_map/psum | solution.py:97
  222.5 0.6 slice_divide_fusion
  223.1 0.6 dynamic_slice.7
  223.7 0.6 dynamic_slice.6
  (17 shorter events, 0.2 us)
Async XLA Ops:
  7.2 76.4 %all-gather.5.cloned.1.call-start = ((), (), s32[]{:S(2)}) async-start(), calls=%async_computation | async-start | bytes 8912896 | tf_op jit(solution)/shard_map/all_gather | solution.py:61
  83.6 78.6 %collective-permute-start.3 = (bf16[16,256,1024]{2,1,0:T(8,128)(2,1)}, bf16[16,256,1024]{2,1,0:T(8,128)(2,1)}, u32[]{:S(2)}, u32[]{:S(2)}) collective-permute-start(bf16[16,256,1024]{2,1,0:T(8,128)(2,1)} %bitcast.97), channel_id=1, source_target_pairs={{0,4},{4,0},{1,5},{5,1},{2,6},{6,2},{3,7},{7,3},{8,12},{12,8},{9,1... | collective-permute-start | bytes 25165832 | tf_op jit(solution)/shard_map/ppermute | solution.py:74
  85.3 15.7 %collective-permute-start.1 = (bf16[1032,256]{1,0:T(8,128)(2,1)S(1)}, bf16[1032,256]{1,0:T(8,128)(2,1)S(1)}, u32[]{:S(2)}, u32[]{:S(2)}) collective-permute-start(bf16[1032,256]{1,0:T(8,128)(2,1)S(1)} %get-tuple-element.40), channel_id=1, source_target_pairs={{0,1},{1,2},{2,3},{3,0},{4,5},{5,6},{6,7},{7,4},{8,9},{9,10},{10,1... | collective-permute-start | bytes 1585160 | tf_op jit(solution)/shard_map/ppermute | solution.py:44
  86.9 14.5 %collective-permute-start = (bf16[1032,256]{1,0:T(8,128)(2,1)S(1)}, bf16[1032,256]{1,0:T(8,128)(2,1)S(1)}, u32[]{:S(2)}, u32[]{:S(2)}) collective-permute-start(bf16[1032,256]{1,0:T(8,128)(2,1)S(1)} %get-tuple-element.40), channel_id=1, source_target_pairs={{0,3},{1,0},{2,1},{3,2},{4,7},{5,4},{6,5},{7,6},{8,11},{9,8},{10,9... | collective-permute-start | bytes 1585160 | tf_op jit(solution)/shard_map/ppermute | solution.py:44
  101.1 14.8 %collective-permute-start.2 = (bf16[1032,256]{1,0:T(8,128)(2,1)S(1)}, bf16[1032,256]{1,0:T(8,128)(2,1)S(1)}, u32[]{:S(2)}, u32[]{:S(2)}) collective-permute-start(bf16[1032,256]{1,0:T(8,128)(2,1)S(1)} %collective-permute-done.1), channel_id=1, source_target_pairs={{0,1},{1,2},{2,3},{3,0},{4,5},{5,6},{6,7},{7,4},{8,9},{9,10},{10,1... | collective-permute-start | bytes 1585160 | tf_op jit(solution)/shard_map/ppermute | solution.py:44
  101.4 14.4 %copy-start.1 = (bf16[1032,256]{1,0:T(8,128)(2,1)}, bf16[1032,256]{1,0:T(8,128)(2,1)S(1)}, u32[]{:S(2)}) copy-start(bf16[1032,256]{1,0:T(8,128)(2,1)S(1)} %collective-permute-done) | copy-start | bytes 1585156
  135.1 2.9 %copy-start = (bf16[1024,4,256]{0,2,1:T(8,128)(2,1)S(1)}, bf16[1024,4,256]{0,2,1:T(8,128)(2,1)}, u32[]{:S(2)}) copy-start(bf16[1024,4,256]{0,2,1:T(8,128)(2,1)} %copy.17) | copy-start | bytes 6291460
  137.9 14.7 %copy-start.2 = (s32[1024]{0:T(1024)S(1)}, s32[1024]{0:T(1024)}, u32[]{:S(2)}) copy-start(s32[1024]{0:T(1024)} %param.11) | copy-start | bytes 12292
Sparse Core Ops, SparseCore 0:
  10.1 73.4 all-gather.4

commit v4 on v2

--- a/solution.py
+++ b/solution.py
@@ -1,6 +1,10 @@
+import functools
+
 import jax
 import jax.numpy as jnp
 from jax import lax
+from jax.experimental import pallas as pl
+from jax.experimental.pallas import tpu as pltpu
 from jax.sharding import Mesh, PartitionSpec as P
 from jax.experimental.layout import Layout, with_layout_constraint
 
@@ -11,15 +15,64 @@
 eps = 1e-06
 
 
-def chunk_stats(normed, piece, vocab_ids, valid, ids):
-    logits = lax.dot_general(normed, piece, (((1,), (1,)), ((), ())), preferred_element_type=jnp.float32)
-    logits = jnp.where(valid[None, :], logits, NEG)
-    top = jnp.max(logits, axis=1)
-    expo = jnp.exp(logits - top[:, None])
-    total = jnp.sum(expo, axis=1)
-    moment = jnp.sum(expo * logits, axis=1)
-    pick = jnp.sum(jnp.where(vocab_ids[None, :] == ids[:, None], logits, 0.0), axis=1)
-    return top, total, moment, pick
+def stats_kernel(steps, x_ref, w_ref, b_ref, top_ref, tot_ref, mom_ref, m_sc, s_sc, mo_sc):
+    j = pl.program_id(1)
+
+    @pl.when(j == 0)
+    def _():
+        m_sc[...] = jnp.full(m_sc.shape, NEG, jnp.float32)
+        s_sc[...] = jnp.zeros(s_sc.shape, jnp.float32)
+        mo_sc[...] = jnp.zeros(mo_sc.shape, jnp.float32)
+
+    logits = lax.dot_general(x_ref[...], w_ref[...], (((1,), (1,)), ((), ())), preferred_element_type=jnp.float32)
+    logits = logits + b_ref[...]
+    m_old = m_sc[...]
+    m_new = jnp.maximum(m_old, jnp.max(logits, axis=1, keepdims=True))
+    e = jnp.exp(logits - m_new)
+    alpha = jnp.exp(m_old - m_new)
+    s_sc[...] = s_sc[...] * alpha + jnp.sum(e, axis=1, keepdims=True)
+    mo_sc[...] = mo_sc[...] * alpha + jnp.sum(e * logits, axis=1, keepdims=True)
+    m_sc[...] = m_new
+
+    @pl.when(j == steps - 1)
+    def _():
+        top_ref[...] = m_sc[...]
+        tot_ref[...] = s_sc[...]
+        mom_ref[...] = mo_sc[...]
+
+
+def fused_stats(normed, piece, bias, tm=512, tn=512):
+    rows, depth = normed.shape
+    cols = piece.shape[0]
+    grid = (rows // tm, cols // tn)
+    stat = jax.ShapeDtypeStruct((rows, 1), jnp.float32)
+    stat_spec = pl.BlockSpec((tm, 1), lambda i, j: (i, 0))
+    return pl.pallas_call(
+        functools.partial(stats_kernel, grid[1]),
+        out_shape=(stat, stat, stat),
+        grid=grid,
+        in_specs=[
+            pl.BlockSpec((tm, depth), lambda i, j: (i, 0)),
+            pl.BlockSpec((tn, depth), lambda i, j: (j, 0)),
+            pl.BlockSpec((1, tn), lambda i, j: (0, j)),
+        ],
+        out_specs=(stat_spec, stat_spec, stat_spec),
+        scratch_shapes=[pltpu.VMEM((tm, 1), jnp.float32)] * 3,
+        compiler_params=pltpu.CompilerParams(dimension_semantics=("arbitrary", "arbitrary")),
+        cost_estimate=pl.CostEstimate(
+            flops=2 * rows * cols * depth,
+            transcendentals=rows * cols,
+            bytes_accessed=2 * (rows * depth + grid[0] * cols * depth),
+        ),
+    )(normed, piece, bias)
+
+
+def chunk_stats(normed, piece, valid, position, found):
+    bias = jnp.where(valid, 0.0, NEG).astype(jnp.float32)[None, :]
+    top, total, moment = fused_stats(normed, piece, bias)
+    rows_of = jnp.take(piece, position, axis=0).astype(jnp.float32)
+    pick = jnp.where(found, jnp.sum(rows_of * normed.astype(jnp.float32), axis=1), 0.0)
+    return top[:, 0], total[:, 0], moment[:, 0], pick
 
 
 def merge(stats):
@@ -71,7 +124,10 @@
         offset = lo + g % chunk
         valid = offset < hi
         vocab_ids = jnp.where(valid, (owner * splits + column_index) * shard_cols + offset, -1)
-        stats.append(chunk_stats(normed, piece, vocab_ids, valid, token_ids))
+        block = token_ids // shard_cols
+        found = block % splits == column_index
+        position = (block // splits) * chunk + token_ids % shard_cols - lo
+        stats.append(chunk_stats(normed, piece, valid, position, found))
     mine = merge(stats)
 
     everyone = lax.all_gather(jnp.stack(mine), "x", axis=0, tiled=False)

time: 175 us -> 209 us (1.19)
  Pallas kernels: 0 us -> 57.6 us
  matrix products: 26.1 us -> 0 us
  local copies, waits for them, and re-layouts: 7.94 us -> 20.1 us
  other arithmetic: 25.1 us -> 16 us
    pallas_call x0 -> x1, Pallas kernels: none -> 57.6 us  [fused_stats(): pl.pallas_call(functools.partial(stats_kernel, grid[1]), out_shape=(stat,...]
    dot_general x1 -> x0, matrix products: 26.1 us -> none  [chunk_stats(): lax.dot_general(normed, piece, (((1,), (1,)), ((), ())), preferred_elemen...]
    reduce_sum x1, other arithmetic: 18 us -> 2.8 us  [chunk_stats(): jnp.sum(rows_of * normed.astype(jnp.float32), axis=1)]
    gather x0 -> x1, local copies, waits for them, and re-layouts: none -> 14 us  [chunk_stats(): rows_of = jnp.take(piece, position, axis=0).astype(jnp.float32)]
    pallas_call x0 -> x3, other arithmetic: none -> 3.74 us  [fused_stats(): pl.pallas_call(functools.partial(stats_kernel, grid[1]), out_shape=(stat,...]
  transfers between devices with their start and end apart: 4 -> 4, of which waited for: 3 -> 3; matrix products, arithmetic and copies ran while one was open for 5% -> 4% of each run, Pallas kernels for 0% -> 0%
where the time goes in v4:
time: 209 us; the launch traced here: 208 us
  waiting for transfers between devices  61.6 us (29%)
  Pallas kernels  57.6 us (28%)
  blocking collectives  33.6 us (16%)
  local copies, waits for them, and re-layouts  20.1 us (10%)
  other arithmetic  16 us (8%)
  between operations  15.5 us (7%)
  starting transfers between devices  3.82 us (2%)
    pallas_call x1, Pallas kernels, fused_stats(): pl.pallas_call(functools.partial(stats_kernel, grid[1]), out_shape=(stat,...  57.6 us
    all_gather x1, waiting for transfers between devices, body(): piece = lax.all_gather(part, REQ, axis=0, tiled=False)  38.4 us
    ppermute x3, waiting for transfers between devices, body(): lax.ppermute(x, 'x', [(i, (i + d) % splits) for i in range(splits)])  23.2 us
    psum x3, blocking collectives, body(): summed = lax.psum(summed, name)  21.4 us
    gather x1, local copies, waits for them, and re-layouts, chunk_stats(): rows_of = jnp.take(piece, position, axis=0).astype(jnp.float32)  14 us
    all_gather x1, blocking collectives, body(): everyone = lax.all_gather(jnp.stack(mine), 'x', axis=0, tiled=False)  12.2 us
  transfers between devices with their start and end apart: 4, of which 3 were waited for; matrix products, arithmetic and copies ran while one was open for 4% of the time, Pallas kernels for 0%

profile of v4, /device:TPU:0, one launch (start us, length us, event | category | flops | bytes accessed | tf_op | source)
XLA Modules:
  0.0 208.1 jit_solution(7113017945266314716)
XLA Ops:
  7.2 0.0 copy-start.3
  7.2 0.0 copy-start.1
  7.2 0.0 copy-start.2
  7.2 0.0 all-gather.5.cloned.1.call-start
  7.2 1.3 copy.19
  8.5 0.8 concatenate.9
  9.4 0.0 all-gather.5.cloned.1.call-update
  9.4 0.0 copy-done.3
  9.4 0.0 copy-done.1
  9.4 0.1 fusion.21
  9.5 1.7 collective-permute-start.1
  11.2 1.6 collective-permute-start
  14.2 0.6 compare_select_fusion.b_ref
  14.8 9.7 %collective-permute-done.1 = bf16[1032,256]{1,0:T(8,128)(2,1)S(1)} collective-permute-done((bf16[1032,256]{1,0:T(8,128)(2,1)S(1)}, bf16[1032,256]{1,0:T(8,128)(2,1)S(1)}, u32[]{:S(2)}, u32[]{:S(2)}) %collective-permute-start.1) | collective-permute-done | bytes 528416 | tf_op jit(solution)/shard_map/ppermute | solution.py:98
  24.5 0.5 collective-permute-start.2
  24.9 0.0 copy-done.2
  25.0 0.0 collective-permute-done
  25.0 0.0 copy-start
  25.0 13.5 %collective-permute-done.2 = bf16[1032,256]{1,0:T(8,128)(2,1)S(1)} collective-permute-done((bf16[1032,256]{1,0:T(8,128)(2,1)S(1)}, bf16[1032,256]{1,0:T(8,128)(2,1)S(1)}, u32[]{:S(2)}, u32[]{:S(2)}) %collective-permute-start.2) | collective-permute-done | bytes 528416 | tf_op jit(solution)/shard_map/ppermute | solution.py:98
  38.5 0.0 copy-done
  38.5 1.3 pad_maximum_fusion
  39.8 2.0 gather_fusion
  41.8 1.9 select_bitcast_fusion
  43.7 0.3 convert_bitcast_fusion
  44.0 0.6 copy.23
  44.7 0.5 fusion
  45.2 1.8 multiply_convert_fusion.x_ref
  47.0 38.4 %all-gather.5.cloned.1.call-done.w_ref = bf16[8192,1024]{1,0:T(8,128)(2,1)} async-done(((bf16[256,1024]{1,0:T(8,128)(2,1)}), bf16[8192,1024]{1,0:T(8,128)(2,1)}) %all-gather.5.cloned.1.call-update) | async-done | bytes 16777232 | tf_op jit(solution)/shard_map/all_gather | solution.py:119
  85.5 57.6 %shard_map.85 = (f32[1024,1]{1,0:T(8,128)}, f32[1024,1]{1,0:T(8,128)}, f32[1024,1]{1,0:T(8,128)}) custom-call(bf16[1024,1024]{1,0:T(8,128)(2,1)} %multiply_convert_fusion.x_ref, bf16[8192,1024]{1,0:T(8,128)(2,1)} %all-gather.5.cloned.1.call-done.w_ref, f32[1,8192]{1,0:T(1,128)} %compare_select_fusion.b_ref), custom_call_target="tpu_custom_call" | custom-call | flops 17179869184 | bytes 35651584 | tf_op jit(solution)/shard_map/pallas_call | solution.py:50
  143.0 1.2 reduce.12
  144.3 1.2 reduce.13
  145.5 1.2 reduce.14
  146.8 14.0 %gather_fusion.1 = bf16[1024,1024]{1,0:T(8,128)(2,1)} fusion(bf16[8192,1024]{1,0:T(8,128)(2,1)} %all-gather.5.cloned.1.call-done.w_ref, s32[1024]{0:T(1024)S(1)} %broadcast_clamp_fusion), kind=kCustom, calls=%fused_computation.1 | custom fusion | bytes 4198400 | tf_op jit(solution)/shard_map/jit(_take)/gather | solution.py:73
  160.7 2.8 %multiply_reduce_fusion = f32[1024]{0:T(1024)S(1)} fusion(bf16[128,4,8,256]{3,2,1,0:T(8,128)(2,1)} %bitcast.68, f32[4,256]{1,0:T(4,128)S(1)} %bitcast.82, f32[1024]{0:T(1024)S(1)} %add_rsqrt_fusion, pred[1024]{0:T(1024)(128)(4,1)S(1)} %get-tuple-element.27, bf16[1032,4,256]{2,0,1:T(8,128)(2,1)S(1)} %select_bitcast_fusion), kind=kLoop, calls=%fused_computation.8 | loop fusion | flops 9436160 | bytes 4207616 | tf_op jit(solution)/shard_map/reduce_sum | solution.py:74
  163.6 12.2 %all-gather.2 = f32[4,4,1024]{2,1,0:T(4,128)S(1)} all-gather(f32[1,4,1024]{2,1,0:T(4,128)S(1)} %maximum_bitcast_fusion), channel_id=3, replica_groups=mesh['y'=4,'z'=4,'c'=2,'x'=4] {'x'}, dimensions={0}, use_global_device_ids=true | all-gather | bytes 81920 | tf_op jit(solution)/shard_map/all_gather | solution.py:133
  175.9 0.1 fusion.7
  175.9 0.6 fusion.22
  176.6 1.4 pad_maximum_fusion.1
  177.9 0.1 broadcast_multiply_fusion
  178.0 2.4 %psum.21 = f32[4,3]{0,1:T(4,128)S(1)} all-reduce(f32[4,3]{0,1:T(4,128)S(1)} %broadcast_multiply_fusion), channel_id=1, replica_groups=mesh['y'=4,'z'=4,'c'=2,'x'=4] {'c'}, use_global_device_ids=true, to_apply=%region_6.7 | all-reduce | flops 12 | bytes 96 | tf_op jit(solution)/shard_map/psum | solution.py:149
  180.4 10.1 %psum.22 = f32[4,3]{0,1:T(4,128)S(1)} all-reduce(f32[4,3]{0,1:T(4,128)S(1)} %psum.21), channel_id=1, replica_groups=mesh['y'=4,'z'=4,'c'=2,'x'=4] {'z'}, use_global_device_ids=true, to_apply=%region_7.8 | all-reduce | flops 12 | bytes 96 | tf_op jit(solution)/shard_map/psum | solution.py:149
  190.5 8.9 %psum.23 = f32[4,3]{0,1:T(4,128)S(1)} all-reduce(f32[4,3]{0,1:T(4,128)S(1)} %psum.22), channel_id=1, replica_groups=mesh['y'=4,'z'=4,'c'=2,'x'=4] {'y'}, use_global_device_ids=true, to_apply=%region_8.9 | all-reduce | flops 12 | bytes 96 | tf_op jit(solution)/shard_map/psum | solution.py:149
  199.4 0.6 slice_divide_fusion
  200.0 0.6 dynamic_slice.7
  200.6 0.6 dynamic_slice.6
  (16 shorter events, 0.2 us)
Async XLA Ops:
  7.2 2.2 %copy-start.3 = (bf16[256]{0:T(256)(128)(2,1)S(1)}, bf16[256]{0:T(256)(128)(2,1)}, u32[]{:S(2)}) copy-start(bf16[256]{0:T(256)(128)(2,1)} %param.9) | copy-start | bytes 1540
  7.2 2.3 %copy-start.1 = (bf16[1024,256]{1,0:T(8,128)(2,1)S(1)}, bf16[1024,256]{1,0:T(8,128)(2,1)}, u32[]{:S(2)}) copy-start(bf16[1024,256]{1,0:T(8,128)(2,1)} %param.8) | copy-start | bytes 1572868
  7.2 17.8 %copy-start.2 = (s32[1024]{0:T(1024)S(1)}, s32[1024]{0:T(1024)}, u32[]{:S(2)}) copy-start(s32[1024]{0:T(1024)} %param.11) | copy-start | bytes 12292
  7.2 78.3 %all-gather.5.cloned.1.call-start = ((), (), s32[]{:S(2)}) async-start(), calls=%async_computation | async-start | bytes 17301504 | tf_op jit(solution)/shard_map/all_gather | solution.py:119
  9.5 15.0 %collective-permute-start.1 = (bf16[1032,256]{1,0:T(8,128)(2,1)S(1)}, bf16[1032,256]{1,0:T(8,128)(2,1)S(1)}, u32[]{:S(2)}, u32[]{:S(2)}) collective-permute-start(bf16[1032,256]{1,0:T(8,128)(2,1)S(1)} %get-tuple-element.30), channel_id=1, source_target_pairs={{0,1},{1,2},{2,3},{3,0},{4,5},{5,6},{6,7},{7,4},{8,9},{9,10},{10,1... | collective-permute-start | bytes 1585160 | tf_op jit(solution)/shard_map/ppermute | solution.py:98
  11.2 13.8 %collective-permute-start = (bf16[1032,256]{1,0:T(8,128)(2,1)S(1)}, bf16[1032,256]{1,0:T(8,128)(2,1)S(1)}, u32[]{:S(2)}, u32[]{:S(2)}) collective-permute-start(bf16[1032,256]{1,0:T(8,128)(2,1)S(1)} %get-tuple-element.30), channel_id=1, source_target_pairs={{0,3},{1,0},{2,1},{3,2},{4,7},{5,4},{6,5},{7,6},{8,11},{9,8},{10,9... | collective-permute-start | bytes 1585160 | tf_op jit(solution)/shard_map/ppermute | solution.py:98
  24.5 14.0 %collective-permute-start.2 = (bf16[1032,256]{1,0:T(8,128)(2,1)S(1)}, bf16[1032,256]{1,0:T(8,128)(2,1)S(1)}, u32[]{:S(2)}, u32[]{:S(2)}) collective-permute-start(bf16[1032,256]{1,0:T(8,128)(2,1)S(1)} %collective-permute-done.1), channel_id=1, source_target_pairs={{0,1},{1,2},{2,3},{3,0},{4,5},{5,6},{6,7},{7,4},{8,9},{9,10},{10,1... | collective-permute-start | bytes 1585160 | tf_op jit(solution)/shard_map/ppermute | solution.py:98
  25.0 13.5 %copy-start = (bf16[1032,256]{1,0:T(8,128)(2,1)}, bf16[1032,256]{1,0:T(8,128)(2,1)S(1)}, u32[]{:S(2)}) copy-start(bf16[1032,256]{1,0:T(8,128)(2,1)S(1)} %collective-permute-done) | copy-start | bytes 1585156
Sparse Core Ops, SparseCore 0:
  10.3 75.1 all-gather.4

commit v5 on v4

--- a/solution.py
+++ b/solution.py
@@ -11,11 +11,12 @@
 PROMPTS = 4
 REQ = ("y", "z", "c")
 NEG = -1e30
+LANES = 128
 
 eps = 1e-06
 
 
-def stats_kernel(steps, x_ref, w_ref, b_ref, top_ref, tot_ref, mom_ref, m_sc, s_sc, mo_sc):
+def stats_kernel(steps, x_ref, w_ref, b_ref, v_ref, t_ref, top_ref, tot_ref, mom_ref, pick_ref, m_sc, s_sc, mo_sc, p_sc):
     j = pl.program_id(1)
 
     @pl.when(j == 0)
@@ -23,25 +24,41 @@
         m_sc[...] = jnp.full(m_sc.shape, NEG, jnp.float32)
         s_sc[...] = jnp.zeros(s_sc.shape, jnp.float32)
         mo_sc[...] = jnp.zeros(mo_sc.shape, jnp.float32)
+        p_sc[...] = jnp.zeros(p_sc.shape, jnp.float32)
 
     logits = lax.dot_general(x_ref[...], w_ref[...], (((1,), (1,)), ((), ())), preferred_element_type=jnp.float32)
     logits = logits + b_ref[...]
+    slabs = logits.shape[1] // LANES
+    lane_max = logits[:, :LANES]
+    for k in range(1, slabs):
+        lane_max = jnp.maximum(lane_max, logits[:, k * LANES:(k + 1) * LANES])
     m_old = m_sc[...]
-    m_new = jnp.maximum(m_old, jnp.max(logits, axis=1, keepdims=True))
-    e = jnp.exp(logits - m_new)
+    m_new = jnp.maximum(m_old, jnp.max(lane_max, axis=1, keepdims=True))
     alpha = jnp.exp(m_old - m_new)
-    s_sc[...] = s_sc[...] * alpha + jnp.sum(e, axis=1, keepdims=True)
-    mo_sc[...] = mo_sc[...] * alpha + jnp.sum(e * logits, axis=1, keepdims=True)
+    s = s_sc[...] * alpha
+    mo = mo_sc[...] * alpha
+    p = p_sc[...]
+    tok = t_ref[...]
+    for k in range(slabs):
+        l = logits[:, k * LANES:(k + 1) * LANES]
+        e = jnp.exp(l - m_new)
+        s = s + e
+        mo = mo + e * l
+        p = p + jnp.where(v_ref[:, k * LANES:(k + 1) * LANES] == tok, l, 0.0)
+    s_sc[...] = s
+    mo_sc[...] = mo
+    p_sc[...] = p
     m_sc[...] = m_new
 
     @pl.when(j == steps - 1)
     def _():
         top_ref[...] = m_sc[...]
-        tot_ref[...] = s_sc[...]
-        mom_ref[...] = mo_sc[...]
+        tot_ref[...] = jnp.sum(s_sc[...], axis=1, keepdims=True)
+        mom_ref[...] = jnp.sum(mo_sc[...], axis=1, keepdims=True)
+        pick_ref[...] = jnp.sum(p_sc[...], axis=1, keepdims=True)
 
 
-def fused_stats(normed, piece, bias, tm=512, tn=512):
+def fused_stats(normed, piece, bias, vocab_ids, ids, tm=512, tn=512):
     rows, depth = normed.shape
     cols = piece.shape[0]
     grid = (rows // tm, cols // tn)
@@ -49,30 +66,30 @@
     stat_spec = pl.BlockSpec((tm, 1), lambda i, j: (i, 0))
     return pl.pallas_call(
         functools.partial(stats_kernel, grid[1]),
-        out_shape=(stat, stat, stat),
+        out_shape=(stat, stat, stat, stat),
         grid=grid,
         in_specs=[
             pl.BlockSpec((tm, depth), lambda i, j: (i, 0)),
             pl.BlockSpec((tn, depth), lambda i, j: (j, 0)),
             pl.BlockSpec((1, tn), lambda i, j: (0, j)),
+            pl.BlockSpec((1, tn), lambda i, j: (0, j)),
+            pl.BlockSpec((tm, 1), lambda i, j: (i, 0)),
         ],
-        out_specs=(stat_spec, stat_spec, stat_spec),
-        scratch_shapes=[pltpu.VMEM((tm, 1), jnp.float32)] * 3,
+        out_specs=(stat_spec, stat_spec, stat_spec, stat_spec),
+        scratch_shapes=[pltpu.VMEM((tm, 1), jnp.float32)] + [pltpu.VMEM((tm, LANES), jnp.float32)] * 3,
         compiler_params=pltpu.CompilerParams(dimension_semantics=("arbitrary", "arbitrary")),
         cost_estimate=pl.CostEstimate(
             flops=2 * rows * cols * depth,
             transcendentals=rows * cols,
             bytes_accessed=2 * (rows * depth + grid[0] * cols * depth),
         ),
-    )(normed, piece, bias)
+    )(normed, piece, bias, vocab_ids, ids)
 
 
-def chunk_stats(normed, piece, valid, position, found):
+def chunk_stats(normed, piece, valid, vocab_ids, ids):
     bias = jnp.where(valid, 0.0, NEG).astype(jnp.float32)[None, :]
-    top, total, moment = fused_stats(normed, piece, bias)
-    rows_of = jnp.take(piece, position, axis=0).astype(jnp.float32)
-    pick = jnp.where(found, jnp.sum(rows_of * normed.astype(jnp.float32), axis=1), 0.0)
-    return top[:, 0], total[:, 0], moment[:, 0], pick
+    top, total, moment, pick = fused_stats(normed, piece, bias, vocab_ids[None, :], ids[:, None])
+    return top[:, 0], total[:, 0], moment[:, 0], pick[:, 0]
 
 
 def merge(stats):
@@ -124,10 +141,7 @@
         offset = lo + g % chunk
         valid = offset < hi
         vocab_ids = jnp.where(valid, (owner * splits + column_index) * shard_cols + offset, -1)
-        block = token_ids // shard_cols
-        found = block % splits == column_index
-        position = (block // splits) * chunk + token_ids % shard_cols - lo
-        stats.append(chunk_stats(normed, piece, valid, position, found))
+        stats.append(chunk_stats(normed, piece, valid, vocab_ids, token_ids))
     mine = merge(stats)
 
     everyone = lax.all_gather(jnp.stack(mine), "x", axis=0, tiled=False)

time: 209 us -> 183 us (0.88)
  local copies, waits for them, and re-layouts: 20.1 us -> 7.11 us
  Pallas kernels: 57.6 us -> 47.4 us
    gather x1 -> x0, local copies, waits for them, and re-layouts: 14 us -> none  [chunk_stats(): rows_of = jnp.take(piece, position, axis=0).astype(jnp.float32)]
    pallas_call x1, Pallas kernels: 57.6 us -> 47.4 us  [fused_stats(): pl.pallas_call(functools.partial(stats_kernel, grid[1]), out_shape=(stat,...]
    reduce_sum x1 -> x0, other arithmetic: 2.8 us -> none  [chunk_stats(): jnp.sum(rows_of * normed.astype(jnp.float32), axis=1)]
    pallas_call x3 -> x4, other arithmetic: 3.74 us -> 4.99 us  [fused_stats(): pl.pallas_call(functools.partial(stats_kernel, grid[1]), out_shape=(stat,...]
  transfers between devices with their start and end apart: 4 -> 4, of which waited for: 3 -> 3; matrix products, arithmetic and copies ran while one was open for 4% -> 6% of each run, Pallas kernels for 0% -> 0%
where the time goes in v5:
time: 183 us; the launch traced here: 182 us
  waiting for transfers between devices  59.9 us (33%)
  Pallas kernels  47.4 us (26%)
  blocking collectives  33.5 us (18%)
  between operations  15.5 us (8%)
  other arithmetic  15.1 us (8%)
  local copies, waits for them, and re-layouts  7.11 us (4%)
  starting transfers between devices  3.82 us (2%)
    pallas_call x1, Pallas kernels, fused_stats(): pl.pallas_call(functools.partial(stats_kernel, grid[1]), out_shape=(stat,...  47.4 us
    all_gather x1, waiting for transfers between devices, body(): piece = lax.all_gather(part, REQ, axis=0, tiled=False)  38.4 us
    ppermute x3, waiting for transfers between devices, body(): lax.ppermute(x, 'x', [(i, (i + d) % splits) for i in range(splits)])  21.5 us
    psum x3, blocking collectives, body(): summed = lax.psum(summed, name)  21.4 us
    all_gather x1, blocking collectives, body(): everyone = lax.all_gather(jnp.stack(mine), 'x', axis=0, tiled=False)  12.2 us
    pallas_call x4, other arithmetic, fused_stats(): pl.pallas_call(functools.partial(stats_kernel, grid[1]), out_shape=(stat,...  4.99 us
    ppermute x3, starting transfers between devices, body(): lax.ppermute(x, 'x', [(i, (i + d) % splits) for i in range(splits)])  3.78 us
  transfers between devices with their start and end apart: 4, of which 3 were waited for; matrix products, arithmetic and copies ran while one was open for 6% of the time, Pallas kernels for 0%

profile of v5, /device:TPU:0, one launch (start us, length us, event | category | flops | bytes accessed | tf_op | source)
XLA Modules:
  0.0 182.3 jit_solution(5926083047906694784)
XLA Ops:
  7.2 0.0 copy-start.3
  7.2 0.0 copy-start.1
  7.2 0.0 copy-start.2
  7.2 0.0 all-gather.5.cloned.1.call-start
  7.2 1.3 copy.18
  8.5 0.8 concatenate.9
  9.4 0.0 all-gather.5.cloned.1.call-update
  9.4 0.0 copy-done.3
  9.4 0.0 copy-done.1
  9.4 0.1 fusion.16
  9.5 1.7 collective-permute-start.1
  11.2 1.6 collective-permute-start
  12.8 0.0 copy-done.2
  12.8 1.0 copy.19.t_ref
  15.2 0.7 compare_select_fusion.v_ref
  15.9 8.6 %collective-permute-done.1 = bf16[1032,256]{1,0:T(8,128)(2,1)S(1)} collective-permute-done((bf16[1032,256]{1,0:T(8,128)(2,1)S(1)}, bf16[1032,256]{1,0:T(8,128)(2,1)S(1)}, u32[]{:S(2)}, u32[]{:S(2)}) %collective-permute-start.1) | collective-permute-done | bytes 528416 | tf_op jit(solution)/shard_map/ppermute | solution.py:115
  24.5 0.5 collective-permute-start.2
  24.9 0.6 compare_select_fusion.1.b_ref
  25.6 0.0 collective-permute-done
  25.6 0.0 copy-start
  25.6 12.9 %collective-permute-done.2 = bf16[1032,256]{1,0:T(8,128)(2,1)S(1)} collective-permute-done((bf16[1032,256]{1,0:T(8,128)(2,1)S(1)}, bf16[1032,256]{1,0:T(8,128)(2,1)S(1)}, u32[]{:S(2)}, u32[]{:S(2)}) %collective-permute-start.2) | collective-permute-done | bytes 528416 | tf_op jit(solution)/shard_map/ppermute | solution.py:115
  38.5 0.0 copy-done
  38.5 1.3 pad_maximum_fusion
  39.8 2.0 %gather_fusion = bf16[4,1032,256]{2,1,0:T(8,128)(2,1)} fusion(bf16[4,1032,256]{2,1,0:T(8,128)(2,1)S(1)} %pad_maximum_fusion, s32[1024]{0:T(1024)S(1)} %pad_clamp_fusion), kind=kCustom, calls=%fused_computation | custom fusion | bytes 4227088 | tf_op jit(solution)/shard_map/jit(_take)/gather | solution.py:121
  41.8 1.9 %select_bitcast_fusion = bf16[1032,4,256]{2,0,1:T(8,128)(2,1)S(1)} fusion(bf16[4,1032,256]{2,1,0:T(8,128)(2,1)} %gather_fusion, pred[4]{0:T(512)(128)(4,1)S(1)} %compare_and_fusion), kind=kLoop, calls=%fused_computation.6 | loop fusion | flops 1056768 | bytes 4227076 | tf_op jit(solution)/shard_map/jit(_take)/select_n | solution.py:121
  43.7 0.3 convert_bitcast_fusion
  44.1 0.6 copy.20
  44.7 0.5 fusion
  45.2 1.8 %multiply_convert_fusion.x_ref = bf16[1024,1024]{1,0:T(8,128)(2,1)} fusion(f32[1024,1024]{1,0:T(8,128)S(1)} %bitcast.60, f32[1024]{0:T(1024)S(1)} %bitcast.71, f32[1024]{0:T(1024)S(1)} %add_rsqrt_fusion), kind=kLoop, calls=%fused_computation.4 | loop fusion | flops 3145728 | bytes 6299648 | tf_op jit(solution)/shard_map/convert_element_type | solution.py:126
  47.0 38.4 %all-gather.5.cloned.1.call-done.w_ref = bf16[8192,1024]{1,0:T(8,128)(2,1)} async-done(((bf16[256,1024]{1,0:T(8,128)(2,1)}), bf16[8192,1024]{1,0:T(8,128)(2,1)}) %all-gather.5.cloned.1.call-update) | async-done | bytes 16777232 | tf_op jit(solution)/shard_map/all_gather | solution.py:136
  85.5 47.4 %shard_map.85 = (f32[1024,1]{1,0:T(8,128)}, f32[1024,1]{1,0:T(8,128)}, f32[1024,1]{1,0:T(8,128)}, f32[1024,1]{1,0:T(8,128)}) custom-call(bf16[1024,1024]{1,0:T(8,128)(2,1)} %multiply_convert_fusion.x_ref, bf16[8192,1024]{1,0:T(8,128)(2,1)} %all-gather.5.cloned.1.call-done.w_ref, f32[1,8192]{1,0:T(1,128)} %compare_select_fusion.1.b_ref, ...), custom_call_target="tpu_custom_call" | custom-call | flops 17179869184 | bytes 35651584 | tf_op jit(solution)/shard_map/pallas_call | solution.py:67
  132.8 1.2 reduce.11
  134.1 1.2 reduce.12
  135.3 1.2 reduce.13
  136.6 1.2 reduce.14
  137.9 12.2 %all-gather.2 = f32[4,4,1024]{2,1,0:T(4,128)S(1)} all-gather(f32[1,4,1024]{2,1,0:T(4,128)S(1)} %maximum_bitcast_fusion), channel_id=3, replica_groups=mesh['y'=4,'z'=4,'c'=2,'x'=4] {'x'}, dimensions={0}, use_global_device_ids=true | all-gather | bytes 81920 | tf_op jit(solution)/shard_map/all_gather | solution.py:147
  150.1 0.1 fusion.9
  150.2 0.6 fusion.17
  150.8 1.4 pad_maximum_fusion.1
  152.2 0.1 broadcast_multiply_fusion
  152.3 2.4 %psum.21 = f32[4,3]{0,1:T(4,128)S(1)} all-reduce(f32[4,3]{0,1:T(4,128)S(1)} %broadcast_multiply_fusion), channel_id=1, replica_groups=mesh['y'=4,'z'=4,'c'=2,'x'=4] {'c'}, use_global_device_ids=true, to_apply=%region_5.6 | all-reduce | flops 12 | bytes 96 | tf_op jit(solution)/shard_map/psum | solution.py:163
  154.7 10.1 %psum.22 = f32[4,3]{0,1:T(4,128)S(1)} all-reduce(f32[4,3]{0,1:T(4,128)S(1)} %psum.21), channel_id=1, replica_groups=mesh['y'=4,'z'=4,'c'=2,'x'=4] {'z'}, use_global_device_ids=true, to_apply=%region_6.7 | all-reduce | flops 12 | bytes 96 | tf_op jit(solution)/shard_map/psum | solution.py:163
  164.8 8.8 %psum.23 = f32[4,3]{0,1:T(4,128)S(1)} all-reduce(f32[4,3]{0,1:T(4,128)S(1)} %psum.22), channel_id=1, replica_groups=mesh['y'=4,'z'=4,'c'=2,'x'=4] {'y'}, use_global_device_ids=true, to_apply=%region_7.8 | all-reduce | flops 12 | bytes 96 | tf_op jit(solution)/shard_map/psum | solution.py:163
  173.7 0.6 slice_divide_fusion
  174.2 0.6 dynamic_slice.7
  174.9 0.6 dynamic_slice.6
  (12 shorter events, 0.2 us)
Async XLA Ops:
  7.2 2.2 %copy-start.3 = (bf16[256]{0:T(256)(128)(2,1)S(1)}, bf16[256]{0:T(256)(128)(2,1)}, u32[]{:S(2)}) copy-start(bf16[256]{0:T(256)(128)(2,1)} %param.9) | copy-start | bytes 1540
  7.2 2.3 %copy-start.1 = (bf16[1024,256]{1,0:T(8,128)(2,1)S(1)}, bf16[1024,256]{1,0:T(8,128)(2,1)}, u32[]{:S(2)}) copy-start(bf16[1024,256]{1,0:T(8,128)(2,1)} %param.8) | copy-start | bytes 1572868
  7.2 5.6 %copy-start.2 = (s32[1024]{0:T(1024)S(1)}, s32[1024]{0:T(1024)}, u32[]{:S(2)}) copy-start(s32[1024]{0:T(1024)} %param.11) | copy-start | bytes 12292
  7.2 78.3 %all-gather.5.cloned.1.call-start = ((), (), s32[]{:S(2)}) async-start(), calls=%async_computation | async-start | bytes 17301504 | tf_op jit(solution)/shard_map/all_gather | solution.py:136
  9.5 15.0 %collective-permute-start.1 = (bf16[1032,256]{1,0:T(8,128)(2,1)S(1)}, bf16[1032,256]{1,0:T(8,128)(2,1)S(1)}, u32[]{:S(2)}, u32[]{:S(2)}) collective-permute-start(bf16[1032,256]{1,0:T(8,128)(2,1)S(1)} %get-tuple-element.30), channel_id=1, source_target_pairs={{0,1},{1,2},{2,3},{3,0},{4,5},{5,6},{6,7},{7,4},{8,9},{9,10},{10,1... | collective-permute-start | bytes 1585160 | tf_op jit(solution)/shard_map/ppermute | solution.py:115
  11.2 14.4 %collective-permute-start = (bf16[1032,256]{1,0:T(8,128)(2,1)S(1)}, bf16[1032,256]{1,0:T(8,128)(2,1)S(1)}, u32[]{:S(2)}, u32[]{:S(2)}) collective-permute-start(bf16[1032,256]{1,0:T(8,128)(2,1)S(1)} %get-tuple-element.30), channel_id=1, source_target_pairs={{0,3},{1,0},{2,1},{3,2},{4,7},{5,4},{6,5},{7,6},{8,11},{9,8},{10,9... | collective-permute-start | bytes 1585160 | tf_op jit(solution)/shard_map/ppermute | solution.py:115
  24.5 14.0 %collective-permute-start.2 = (bf16[1032,256]{1,0:T(8,128)(2,1)S(1)}, bf16[1032,256]{1,0:T(8,128)(2,1)S(1)}, u32[]{:S(2)}, u32[]{:S(2)}) collective-permute-start(bf16[1032,256]{1,0:T(8,128)(2,1)S(1)} %collective-permute-done.1), channel_id=1, source_target_pairs={{0,1},{1,2},{2,3},{3,0},{4,5},{5,6},{6,7},{7,4},{8,9},{9,10},{10,1... | collective-permute-start | bytes 1585160 | tf_op jit(solution)/shard_map/ppermute | solution.py:115
  25.6 12.9 %copy-start = (bf16[1032,256]{1,0:T(8,128)(2,1)}, bf16[1032,256]{1,0:T(8,128)(2,1)S(1)}, u32[]{:S(2)}) copy-start(bf16[1032,256]{1,0:T(8,128)(2,1)S(1)} %collective-permute-done) | copy-start | bytes 1585156
Sparse Core Ops, SparseCore 0:
  10.3 75.1 all-gather.4
